TPU v7x, 32 devices: a whole 2x2x4 slice. The times are simulated.
32 devices in a mesh: dp: 2 (over core), ctx: 4 (over z), tp: 4 (over y, x).
Axes of the slice: x: 2, y: 2, z: 4, core: 2. Of those that a mesh axis runs over, the one named last changes fastest.
Arguments:
- inputs: float32 [6, 1024, 768], P('dp', 'ctx'), may hold values from -6 to 6
- encoder_out: bfloat16 [6, 1024, 768], P('dp', 'ctx'), may hold values from -6 to 6
- segments: int32 [6, 1024], P('dp', 'ctx'), may hold values from 0 to 2, never falling along the last dimension, each value on 1 to 512 neighbouring positions
- encoder_segments: int32 [6, 1024], P('dp', 'ctx'), may hold values from 0 to 2, never falling along the last dimension, each value on 1 to 512 neighbouring positions
- self_gain: bfloat16 [768], P(('dp', 'ctx')), may hold values from 0.5 to 1.5
- w_query: bfloat16 [768, 768], P(('dp', 'ctx'), 'tp'), may hold values from -0.0546875 to 0.0546875
- w_key: bfloat16 [768, 768], P(('dp', 'ctx'), 'tp'), may hold values from -0.21875 to 0.21875
- w_value: bfloat16 [768, 768], P(('dp', 'ctx'), 'tp'), may hold values from -0.21875 to 0.21875
- w_out: bfloat16 [768, 768], P('tp', ('dp', 'ctx')), may hold values from -1.75 to 1.75
- relative_bucket_bias: float32 [32, 12], P(None, 'tp'), may hold values from -2 to 2
- cross_gain: bfloat16 [768], P(('dp', 'ctx')), may hold values from 0.5 to 1.5
- cw_query: bfloat16 [768, 768], P(('dp', 'ctx'), 'tp'), may hold values from -0.0546875 to 0.0546875
- cw_key: bfloat16 [768, 768], P(('dp', 'ctx'), 'tp'), may hold values from -0.21875 to 0.21875
- cw_value: bfloat16 [768, 768], P(('dp', 'ctx'), 'tp'), may hold values from -0.21875 to 0.21875
- cw_out: bfloat16 [768, 768], P('tp', ('dp', 'ctx')), may hold values from -1.75 to 1.75
- ff_gain: bfloat16 [768], P(('dp', 'ctx')), may hold values from 0.5 to 1.5
- w_gate: bfloat16 [768, 2048], P(('dp', 'ctx'), 'tp'), may hold values from -0.21875 to 0.21875
- w_up: bfloat16 [768, 2048], P(('dp', 'ctx'), 'tp'), may hold values from -0.21875 to 0.21875
- w_down: bfloat16 [2048, 768], P('tp', ('dp', 'ctx')), may hold values from -0.125 to 0.125
- cotangent: float32 [6, 1024, 768], P('dp', 'ctx'), may hold values from -6 to 6
Outputs:
- outputs: float32 [6, 1024, 768], P('dp', 'ctx')
- d_inputs: float32 [6, 1024, 768], P('dp', 'ctx')
- d_encoded: float32 [6, 1024, 768], P('dp', 'ctx')
- d_self_gain: float32 [768], P(('dp', 'ctx'))
- d_w_query: float32 [768, 768], P(('dp', 'ctx'), 'tp')
- d_w_key: float32 [768, 768], P(('dp', 'ctx'), 'tp')
- d_w_value: float32 [768, 768], P(('dp', 'ctx'), 'tp')
- d_w_out: float32 [768, 768], P('tp', ('dp', 'ctx'))
- d_rel_bias: float32 [32, 12], P(None, 'tp')
- d_cross_gain: float32 [768], P(('dp', 'ctx'))
- d_cw_query: float32 [768, 768], P(('dp', 'ctx'), 'tp')
- d_cw_key: float32 [768, 768], P(('dp', 'ctx'), 'tp')
- d_cw_value: float32 [768, 768], P(('dp', 'ctx'), 'tp')
- d_cw_out: float32 [768, 768], P('tp', ('dp', 'ctx'))
- d_ff_gain: float32 [768], P(('dp', 'ctx'))
- d_w_gate: float32 [768, 2048], P(('dp', 'ctx'), 'tp')
- d_w_up: float32 [768, 2048], P(('dp', 'ctx'), 'tp')
- d_w_down: float32 [2048, 768], P('tp', ('dp', 'ctx'))
Inputs may be any that keep to these rules, and one draw needn't show every extreme that they name: `segments`: in every sequence the numbers never fall, every number 0 to 2 occurs, no document has more than 512 tokens and one has exactly that many. `encoder_segments`: in every sequence the numbers never fall, every number 0 to 2 occurs, no run has more than 512 outputs and one has exactly that many.
All inputs are finite; a program needn't handle non-finite values.
Results may differ from a plain program's by a relative error of at most 0.023.
The roundings to bfloat16 on the way count: a program that leaves them out, or rounds other values in their place, can miss the bound.
Values may be sent and summed in bfloat16 or wider, within the bound.
No kernel may reach another device: no remote copies, remote signals or barrier semaphores. Data moves between devices by JAX's collectives and lax.ppermute only.
A program may use at most 192 MiB of HBM per device.

v0:
```python
import jax
import jax.numpy as jnp
import numpy as np
from jax import lax
from jax.sharding import PartitionSpec as P

HEAD_DIM = 64
NB = 32
MB = 3


EPS = 1e-06
NEG = -1e30
FULL_PRECISION = lax.Precision.HIGHEST
bucket_edges = [int(np.ceil(16.0 * 8.0 ** (slot_index / 16.0))) for slot_index in range(1, 16)]


def rms_norm(values, gain_vec):
    inv_root = lax.rsqrt(jnp.mean(values * values, axis=-1, keepdims=True) + EPS)
    return values * inv_root * gain_vec


def gated_gelu(gate_pre, up_pre):
    return jax.nn.gelu(gate_pre, approximate=True) * up_pre


def bucket_index(distance):
    clipped = jnp.maximum(distance, 0)
    result = jnp.minimum(clipped, 16)
    for edge_value in bucket_edges:
        result = result + (clipped >= edge_value).astype(jnp.int32)
    return result


def bias_table(relative_bucket_bias, distance):
    bucket_indicator = (
        bucket_index(distance)[None] == jnp.arange(NB, dtype=jnp.int32)[:, None, None]
    ).astype(jnp.float32)
    return (
        bucket_indicator,
        jnp.einsum("sz,snl->znl", relative_bucket_bias, bucket_indicator, precision=FULL_PRECISION)[
            None
        ],
    )


def project(left_rows, weight):
    return jnp.einsum("std,dh->sth", left_rows, weight, preferred_element_type=jnp.float32)


def project_back(grad_rows, weight):
    return jnp.einsum("sth,dh->std", grad_rows, weight, preferred_element_type=jnp.float32)


def weight_grad(left_rows, grad_rows):
    return jnp.einsum("std,sth->dh", left_rows, grad_rows, preferred_element_type=jnp.float32)


def masked_scores(queries, keys, allowed, pos_bias):
    raw_scores = jnp.einsum("sqhe,skhe->shqk", queries, keys, preferred_element_type=jnp.float32)
    return jnp.where(allowed, raw_scores + pos_bias, NEG)


def softmax_rows(scores):
    row_top = jnp.max(scores, axis=-1, keepdims=True)
    exp_scores = jnp.exp(scores - row_top)
    row_total = jnp.sum(exp_scores, axis=-1, keepdims=True)
    return (exp_scores / row_total, row_top + jnp.log(row_total))


def weighted_sum(prob_rows, values):
    low_probs = prob_rows.astype(jnp.bfloat16)
    return jnp.einsum("shqk,skhe->sqhe", low_probs, values, preferred_element_type=jnp.float32)


def attention_back(scores, log_total, grad_heads, queries, keys, values):
    prob_rows = jnp.exp(scores - log_total)
    dprob_rows = jnp.einsum(
        "sqhe,skhe->shqk", grad_heads, values, preferred_element_type=jnp.float32
    )
    row_inner = jnp.sum(prob_rows * dprob_rows, axis=-1, keepdims=True)
    dscore = prob_rows * (dprob_rows - row_inner)
    low_score = dscore.astype(jnp.bfloat16)
    grad_query = jnp.einsum("shqk,skhe->sqhe", low_score, keys, preferred_element_type=jnp.float32)
    grad_key = jnp.einsum("shqk,sqhe->skhe", low_score, queries, preferred_element_type=jnp.float32)
    grad_value = jnp.einsum(
        "shqk,sqhe->skhe",
        prob_rows.astype(jnp.bfloat16),
        grad_heads,
        preferred_element_type=jnp.float32,
    )
    return (dscore, grad_query, grad_key, grad_value, row_inner)


def branch_sum(partial_rows):
    return lax.psum(partial_rows, "tp")


def input_sum(partial_rows):
    return lax.psum(partial_rows, "tp")


def scatter_total(parts):
    return (
        lax.psum_scatter(parts[0], ("dp", "ctx"), scatter_dimension=0, tiled=True),
        lax.psum_scatter(parts[1], ("dp", "ctx"), scatter_dimension=0, tiled=True),
        lax.psum_scatter(parts[2], ("dp", "ctx"), scatter_dimension=0, tiled=True),
        lax.psum_scatter(parts[3], ("dp", "ctx"), scatter_dimension=0, tiled=True),
        lax.psum_scatter(parts[4], ("dp", "ctx"), scatter_dimension=0, tiled=True),
        lax.psum_scatter(parts[5], ("dp", "ctx"), scatter_dimension=0, tiled=True),
        lax.psum_scatter(parts[6], ("dp", "ctx"), scatter_dimension=0, tiled=True),
        lax.psum_scatter(parts[7], ("dp", "ctx"), scatter_dimension=0, tiled=True),
        lax.psum_scatter(parts[8], ("dp", "ctx"), scatter_dimension=0, tiled=True),
        lax.psum_scatter(parts[9], ("dp", "ctx"), scatter_dimension=0, tiled=True),
        lax.psum_scatter(parts[10], ("dp", "ctx"), scatter_dimension=0, tiled=True),
        lax.psum_scatter(parts[11], ("dp", "ctx"), scatter_dimension=1, tiled=True),
        lax.psum_scatter(parts[12], ("dp", "ctx"), scatter_dimension=1, tiled=True),
        lax.psum_scatter(parts[13], ("dp", "ctx"), scatter_dimension=1, tiled=True),
    )


def per_device(
    inputs,
    encoder_out,
    segments,
    encoder_segments,
    self_gain,
    w_query,
    w_key,
    w_value,
    w_out,
    relative_bucket_bias,
    cross_gain,
    cw_query,
    cw_key,
    cw_value,
    cw_out,
    ff_gain,
    w_gate,
    w_up,
    w_down,
    cotangent,
):
    ctx_count = lax.axis_size("ctx")
    ctx_place = lax.axis_index("ctx")
    seq_here = inputs.shape[0]
    local_rows = inputs.shape[1]
    enc_rows = encoder_out.shape[1]
    length = local_rows * ctx_count
    enc_length = enc_rows * ctx_count
    heads_here = w_query.shape[1] // HEAD_DIM
    per_batch = seq_here // MB
    fetched = (
        lax.all_gather(self_gain, ("dp", "ctx"), axis=0, tiled=True),
        lax.all_gather(cross_gain, ("dp", "ctx"), axis=0, tiled=True),
        lax.all_gather(ff_gain, ("dp", "ctx"), axis=0, tiled=True),
        lax.all_gather(w_query, ("dp", "ctx"), axis=0, tiled=True),
        lax.all_gather(w_key, ("dp", "ctx"), axis=0, tiled=True),
        lax.all_gather(w_value, ("dp", "ctx"), axis=0, tiled=True),
        lax.all_gather(cw_query, ("dp", "ctx"), axis=0, tiled=True),
        lax.all_gather(cw_key, ("dp", "ctx"), axis=0, tiled=True),
        lax.all_gather(cw_value, ("dp", "ctx"), axis=0, tiled=True),
        lax.all_gather(w_gate, ("dp", "ctx"), axis=0, tiled=True),
        lax.all_gather(w_up, ("dp", "ctx"), axis=0, tiled=True),
        lax.all_gather(w_out, ("dp", "ctx"), axis=1, tiled=True),
        lax.all_gather(cw_out, ("dp", "ctx"), axis=1, tiled=True),
        lax.all_gather(w_down, ("dp", "ctx"), axis=1, tiled=True),
    )
    gain_one = fetched[0].astype(jnp.float32)
    gain_two = fetched[1].astype(jnp.float32)
    gain_three = fetched[2].astype(jnp.float32)
    full_query, full_key, full_value = (fetched[3], fetched[4], fetched[5])
    full_cquery, full_ckey, full_cvalue = (fetched[6], fetched[7], fetched[8])
    full_gate, full_up = (fetched[9], fetched[10])
    full_out, full_cout, full_down = (fetched[11], fetched[12], fetched[13])
    query_pos = ctx_place * local_rows + jnp.arange(local_rows, dtype=jnp.int32)
    key_pos = jnp.arange(length, dtype=jnp.int32)
    distance = query_pos[:, None] - key_pos[None, :]
    causal = distance >= 0
    bucket_indicator, pos_bias = bias_table(relative_bucket_bias, distance)
    totals = [jnp.zeros(member.shape, jnp.float32) for member in fetched]
    bias_total = jnp.zeros(relative_bucket_bias.shape, jnp.float32)
    output_list = []
    dinput_list = []
    dencoded_list = []
    for batch_index in range(MB):
        seq_start = batch_index * per_batch
        resid_in = inputs[seq_start : seq_start + per_batch]
        seg_local = segments[seq_start : seq_start + per_batch]
        enc_local = encoder_out[seq_start : seq_start + per_batch]
        eseg_local = encoder_segments[seq_start : seq_start + per_batch]
        act_one = rms_norm(resid_in, gain_one).astype(jnp.bfloat16)
        query_low = project(act_one, full_query).astype(jnp.bfloat16)
        key_local = project(act_one, full_key).astype(jnp.bfloat16)
        value_local = project(act_one, full_value).astype(jnp.bfloat16)
        key_all, value_all, seg_all = (
            lax.all_gather(key_local, "ctx", axis=1, tiled=True),
            lax.all_gather(value_local, "ctx", axis=1, tiled=True),
            lax.all_gather(seg_local, "ctx", axis=1, tiled=True),
        )
        allowed = (causal[None] & (seg_local[:, :, None] == seg_all[:, None, :]))[:, None]
        query_heads = query_low.reshape(per_batch, local_rows, heads_here, HEAD_DIM)
        key_heads = key_all.reshape(per_batch, length, heads_here, HEAD_DIM)
        value_heads = value_all.reshape(per_batch, length, heads_here, HEAD_DIM)
        self_probs, self_lse = softmax_rows(
            masked_scores(query_heads, key_heads, allowed, pos_bias)
        )
        att_low = (
            weighted_sum(self_probs, value_heads)
            .reshape(per_batch, local_rows, -1)
            .astype(jnp.bfloat16)
        )
        resid_one = resid_in + branch_sum(project(att_low, full_out))
        act_two = rms_norm(resid_one, gain_two).astype(jnp.bfloat16)
        cquery = project(act_two, full_cquery).astype(jnp.bfloat16)
        ckey_local = project(enc_local, full_ckey).astype(jnp.bfloat16)
        cvalue_local = project(enc_local, full_cvalue).astype(jnp.bfloat16)
        ckey_all, cvalue_all, eseg_all = (
            lax.all_gather(ckey_local, "ctx", axis=1, tiled=True),
            lax.all_gather(cvalue_local, "ctx", axis=1, tiled=True),
            lax.all_gather(eseg_local, "ctx", axis=1, tiled=True),
        )
        cross_allowed = (seg_local[:, :, None] == eseg_all[:, None, :])[:, None]
        cquery_heads = cquery.reshape(per_batch, local_rows, heads_here, HEAD_DIM)
        ckey_heads = ckey_all.reshape(per_batch, enc_length, heads_here, HEAD_DIM)
        cvalue_heads = cvalue_all.reshape(per_batch, enc_length, heads_here, HEAD_DIM)
        cross_probs, cross_lse = softmax_rows(
            masked_scores(cquery_heads, ckey_heads, cross_allowed, 0.0)
        )
        catt_low = (
            weighted_sum(cross_probs, cvalue_heads)
            .reshape(per_batch, local_rows, -1)
            .astype(jnp.bfloat16)
        )
        resid_two = resid_one + branch_sum(project(catt_low, full_cout))
        act_three = rms_norm(resid_two, gain_three).astype(jnp.bfloat16)
        gate_pre = project(act_three, full_gate)
        up_pre = project(act_three, full_up)
        hidden = gated_gelu(gate_pre, up_pre).astype(jnp.bfloat16)
        output_list.append(resid_two + branch_sum(project(hidden, full_down)))
        step_grads = [None] * 14
        grad_out = cotangent[seq_start : seq_start + per_batch]
        g_ff = grad_out.astype(jnp.bfloat16)
        step_grads[13] = weight_grad(hidden, g_ff)
        d_hidden = project_back(g_ff, full_down)
        d_gate, d_up = jax.vjp(gated_gelu, gate_pre, up_pre)[1](d_hidden)
        d_gate = d_gate.astype(jnp.bfloat16)
        d_up = d_up.astype(jnp.bfloat16)
        step_grads[9] = weight_grad(act_three, d_gate)
        step_grads[10] = weight_grad(act_three, d_up)
        d_act_three = input_sum(project_back(d_gate, full_gate) + project_back(d_up, full_up))
        norm_three, step_grads[2] = jax.vjp(rms_norm, resid_two, gain_three)[1](d_act_three)
        grad_two = grad_out + norm_three
        g_cross = grad_two.astype(jnp.bfloat16)
        step_grads[12] = weight_grad(catt_low, g_cross)
        d_catt = (
            project_back(g_cross, full_cout)
            .astype(jnp.bfloat16)
            .reshape(per_batch, local_rows, heads_here, HEAD_DIM)
        )
        cross_recomputed = masked_scores(cquery_heads, ckey_heads, cross_allowed, 0.0)
        cross_dscore, d_cquery, d_ckey, d_cvalue, cross_inner = attention_back(
            cross_recomputed, cross_lse, d_catt, cquery_heads, ckey_heads, cvalue_heads
        )
        d_ckey_local, d_cvalue_local = (
            lax.psum_scatter(
                d_ckey.reshape(per_batch, enc_length, -1), "ctx", scatter_dimension=1, tiled=True
            ),
            lax.psum_scatter(
                d_cvalue.reshape(per_batch, enc_length, -1), "ctx", scatter_dimension=1, tiled=True
            ),
        )
        d_ckey_low = d_ckey_local.astype(jnp.bfloat16)
        d_cvalue_low = d_cvalue_local.astype(jnp.bfloat16)
        d_cquery_low = d_cquery.reshape(per_batch, local_rows, -1).astype(jnp.bfloat16)
        step_grads[6] = weight_grad(act_two, d_cquery_low)
        step_grads[7] = weight_grad(enc_local, d_ckey_low)
        step_grads[8] = weight_grad(enc_local, d_cvalue_low)
        d_act_two = project_back(d_cquery_low, full_cquery)
        d_enc_part = project_back(d_ckey_low, full_ckey) + project_back(d_cvalue_low, full_cvalue)
        joined = input_sum(jnp.concatenate([d_act_two, d_enc_part], axis=1))
        dencoded_list.append(joined[:, local_rows:])
        second_norm, step_grads[1] = jax.vjp(rms_norm, resid_one, gain_two)[1](
            joined[:, :local_rows]
        )
        grad_one = grad_two + second_norm
        g_self = grad_one.astype(jnp.bfloat16)
        step_grads[11] = weight_grad(att_low, g_self)
        d_att_rows = project_back(g_self, full_out).astype(jnp.bfloat16)
        d_att = d_att_rows.reshape(per_batch, local_rows, heads_here, HEAD_DIM)
        key_back, value_back = (
            lax.all_gather(key_local, "ctx", axis=1, tiled=True),
            lax.all_gather(value_local, "ctx", axis=1, tiled=True),
        )
        key_heads_back = key_back.reshape(per_batch, length, heads_here, HEAD_DIM)
        value_heads_back = value_back.reshape(per_batch, length, heads_here, HEAD_DIM)
        self_again = masked_scores(query_heads, key_heads_back, allowed, pos_bias)
        self_score_gradient, d_query, d_key, d_value, self_inner = attention_back(
            self_again, self_lse, d_att, query_heads, key_heads_back, value_heads_back
        )
        bias_step = jnp.einsum(
            "vcz,ecz->ev",
            jnp.sum(self_score_gradient, axis=0),
            bucket_indicator,
            precision=FULL_PRECISION,
        )
        d_key_local, d_value_local = (
            lax.psum_scatter(
                d_key.reshape(per_batch, length, -1), "ctx", scatter_dimension=1, tiled=True
            ),
            lax.psum_scatter(
                d_value.reshape(per_batch, length, -1), "ctx", scatter_dimension=1, tiled=True
            ),
        )
        d_key_low = d_key_local.astype(jnp.bfloat16)
        d_value_low = d_value_local.astype(jnp.bfloat16)
        d_query_low = d_query.reshape(per_batch, local_rows, -1).astype(jnp.bfloat16)
        step_grads[3] = weight_grad(act_one, d_query_low)
        step_grads[4] = weight_grad(act_one, d_key_low)
        step_grads[5] = weight_grad(act_one, d_value_low)
        d_act_one = input_sum(
            project_back(d_query_low, full_query)
            + project_back(d_key_low, full_key)
            + project_back(d_value_low, full_value)
        )
        norm_one, step_grads[0] = jax.vjp(rms_norm, resid_in, gain_one)[1](d_act_one)
        dinput_list.append(grad_one + norm_one)
        totals = [running + fresh for running, fresh in zip(totals, step_grads)]
        bias_total = bias_total + bias_step
    final_grads = scatter_total(totals)
    bias_final = lax.psum(bias_total, ("dp", "ctx"))
    return (
        jnp.concatenate(output_list, axis=0),
        jnp.concatenate(dinput_list, axis=0),
        jnp.concatenate(dencoded_list, axis=0),
        final_grads[0],
        final_grads[3],
        final_grads[4],
        final_grads[5],
        final_grads[11],
        bias_final,
        final_grads[1],
        final_grads[6],
        final_grads[7],
        final_grads[8],
        final_grads[12],
        final_grads[2],
        final_grads[9],
        final_grads[10],
        final_grads[13],
    )


def solution(mesh):
    placed = (
        P("dp", "ctx", None),
        P("dp", "ctx", None),
        P("dp", "ctx"),
        P("dp", "ctx"),
        P(("dp", "ctx")),
        P(("dp", "ctx"), "tp"),
        P(("dp", "ctx"), "tp"),
        P(("dp", "ctx"), "tp"),
        P("tp", ("dp", "ctx")),
        P(None, "tp"),
        P(("dp", "ctx")),
        P(("dp", "ctx"), "tp"),
        P(("dp", "ctx"), "tp"),
        P(("dp", "ctx"), "tp"),
        P("tp", ("dp", "ctx")),
        P(("dp", "ctx")),
        P(("dp", "ctx"), "tp"),
        P(("dp", "ctx"), "tp"),
        P("tp", ("dp", "ctx")),
        P("dp", "ctx", None),
    )
    return jax.shard_map(
        per_device,
        mesh=mesh,
        in_specs=placed,
        out_specs=(
            P("dp", "ctx", None),
            P("dp", "ctx", None),
            P("dp", "ctx", None),
            P(("dp", "ctx")),
            P(("dp", "ctx"), "tp"),
            P(("dp", "ctx"), "tp"),
            P(("dp", "ctx"), "tp"),
            P("tp", ("dp", "ctx")),
            P(None, "tp"),
            P(("dp", "ctx")),
            P(("dp", "ctx"), "tp"),
            P(("dp", "ctx"), "tp"),
            P(("dp", "ctx"), "tp"),
            P("tp", ("dp", "ctx")),
            P(("dp", "ctx")),
            P(("dp", "ctx"), "tp"),
            P(("dp", "ctx"), "tp"),
            P("tp", ("dp", "ctx")),
        ),
        check_vma=False,
    )
```

profile of v0, /device:TPU:0, one launch (start us, length us, event | category | flops | bytes accessed | tf_op | source)
XLA Modules:
  0.0 1704.1 jit_solution(2302931716532765954)
XLA Ops:
  33.8 26.2 %all_gather.120 = bf16[768,192]{1,0:T(8,128)(2,1)S(1)} all-gather(bf16[96,192]{1,0:T(8,128)(2,1)} %param.26), channel_id=1, replica_groups=mesh['dp'=2,'ctx'=4,'tp'=4] {'dp','ctx'}, dimensions={0}, use_global_device_ids=true | all-gather | bytes 331776 | tf_op jit(solution)/shard_map/all_gather | solution.py:158
  60.1 26.3 %all_gather.119 = bf16[768,192]{1,0:T(8,128)(2,1)S(1)} all-gather(bf16[96,192]{1,0:T(8,128)(2,1)} %param.25), channel_id=1, replica_groups=mesh['dp'=2,'ctx'=4,'tp'=4] {'dp','ctx'}, dimensions={0}, use_global_device_ids=true | all-gather | bytes 331776 | tf_op jit(solution)/shard_map/all_gather | solution.py:157
  89.3 26.2 %all_gather.115 = bf16[768,192]{1,0:T(8,128)(2,1)S(1)} all-gather(bf16[96,192]{1,0:T(8,128)(2,1)S(1)} %copy-done.176), channel_id=1, replica_groups=mesh['dp'=2,'ctx'=4,'tp'=4] {'dp','ctx'}, dimensions={0}, use_global_device_ids=true | all-gather | bytes 331776 | tf_op jit(solution)/shard_map/all_gather | solution.py:159
  203.6 24.7 %all_gather.122 = bf16[192,768]{0,1:T(8,128)(2,1)S(1)} all-gather(bf16[192,96]{0,1:T(8,128)(2,1)S(1)} %copy.45), channel_id=1, replica_groups=mesh['dp'=2,'ctx'=4,'tp'=4] {'dp','ctx'}, dimensions={1}, use_global_device_ids=true | all-gather | bytes 331776 | tf_op jit(solution)/shard_map/all_gather | solution.py:165
  317.2 27.2 %all_gather.128 = bf16[768,192]{1,0:T(8,128)(2,1)} all-gather(bf16[96,192]{1,0:T(8,128)(2,1)} %param.31), channel_id=1, replica_groups=mesh['dp'=2,'ctx'=4,'tp'=4] {'dp','ctx'}, dimensions={0}, use_global_device_ids=true | all-gather | bytes 331776 | tf_op jit(solution)/shard_map/all_gather | solution.py:160
  344.3 27.0 %all_gather.129 = bf16[768,192]{1,0:T(8,128)(2,1)} all-gather(bf16[96,192]{1,0:T(8,128)(2,1)} %param.32), channel_id=1, replica_groups=mesh['dp'=2,'ctx'=4,'tp'=4] {'dp','ctx'}, dimensions={0}, use_global_device_ids=true | all-gather | bytes 331776 | tf_op jit(solution)/shard_map/all_gather | solution.py:161
  371.3 27.1 %all_gather.123 = bf16[768,192]{1,0:T(8,128)(2,1)} all-gather(bf16[96,192]{1,0:T(8,128)(2,1)} %param.33), channel_id=1, replica_groups=mesh['dp'=2,'ctx'=4,'tp'=4] {'dp','ctx'}, dimensions={0}, use_global_device_ids=true | all-gather | bytes 331776 | tf_op jit(solution)/shard_map/all_gather | solution.py:162
  400.0 27.1 %all_gather.131 = bf16[192,768]{0,1:T(8,128)(2,1)} all-gather(bf16[192,96]{0,1:T(8,128)(2,1)} %copy.46), channel_id=1, replica_groups=mesh['dp'=2,'ctx'=4,'tp'=4] {'dp','ctx'}, dimensions={1}, use_global_device_ids=true | all-gather | bytes 331776 | tf_op jit(solution)/shard_map/all_gather | solution.py:166
  542.3 30.0 %all_gather.133 = bf16[768,512]{1,0:T(8,128)(2,1)} all-gather(bf16[96,512]{1,0:T(8,128)(2,1)} %param.36), channel_id=1, replica_groups=mesh['dp'=2,'ctx'=4,'tp'=4] {'dp','ctx'}, dimensions={0}, use_global_device_ids=true | all-gather | bytes 884736 | tf_op jit(solution)/shard_map/all_gather | solution.py:163
  572.3 29.8 %all_gather.134 = bf16[768,512]{1,0:T(8,128)(2,1)} all-gather(bf16[96,512]{1,0:T(8,128)(2,1)} %param.37), channel_id=1, replica_groups=mesh['dp'=2,'ctx'=4,'tp'=4] {'dp','ctx'}, dimensions={0}, use_global_device_ids=true | all-gather | bytes 884736 | tf_op jit(solution)/shard_map/all_gather | solution.py:164
  602.1 30.7 %all_gather.135 = bf16[512,768]{0,1:T(8,128)(2,1)} all-gather(bf16[512,96]{0,1:T(8,128)(2,1)} %param.38), channel_id=1, replica_groups=mesh['dp'=2,'ctx'=4,'tp'=4] {'dp','ctx'}, dimensions={1}, use_global_device_ids=true | all-gather | bytes 884736 | tf_op jit(solution)/shard_map/all_gather | solution.py:167
  650.9 74.7 %all-reduce.23.cloned.1.call-done = (f32[1,256,768]{2,1,0:T(8,128)}, f32[1,256,768]{2,1,0:T(8,128)}, f32[1,256,768]{2,1,0:T(8,128)}) async-done(((f32[1,256,768]{2,1,0:T(8,128)}, f32[1,256,768]{2,1,0:T(8,128)}, f32[1,256,768]{2,1,0:T(8,128)}), (f32[1,256,768]{2,1,0:T(8,128)}, f32[1,256,768]{2,1,0:T(8,128)}, f32[1,256,768]{2,1,0:T(8,128)})) %all-reduce.23.cloned.1.call-update) | async-done | bytes 2359312 | tf_op jit(solution)/shard_map/psum | solution.py:100
  813.9 22.8 %reduce-scatter.42.cloned.1.call-done = f32[1,256,192]{1,2,0:T(8,128)} async-done(((f32[1,1024,192]{1,2,0:T(8,128)}), f32[1,256,192]{1,2,0:T(8,128)}) %reduce-scatter.42.cloned.1.call-update) | async-done | bytes 196624 | tf_op jit(solution)/shard_map/reduce_scatter | solution.py:269
  892.1 111.7 %all-reduce.21.cloned.1.call-done = (f32[1,512,768]{2,1,0:T(8,128)}, f32[1,512,768]{2,1,0:T(8,128)}, f32[1,512,768]{2,1,0:T(8,128)}) async-done(((f32[1,512,768]{2,1,0:T(8,128)}, f32[1,512,768]{2,1,0:T(8,128)}, f32[1,512,768]{2,1,0:T(8,128)}), (f32[1,512,768]{2,1,0:T(8,128)}, f32[1,512,768]{2,1,0:T(8,128)}, f32[1,512,768]{2,1,0:T(8,128)})) %all-reduce.21.cloned.1.call-update) | async-done | bytes 4718608 | tf_op jit(solution)/shard_map/psum | solution.py:100
  1286.2 69.2 %all-reduce.19.cloned.1.call-done = (f32[1,256,768]{2,1,0:T(8,128)}, f32[1,256,768]{2,1,0:T(8,128)}, f32[1,256,768]{2,1,0:T(8,128)}, f32[1,256,768]{2,1,0:T(8,12...) async-done(((f32[1,256,768]{2,1,0:T(8,128)}, f32[1,256,768]{2,1,0:T(8,128)}, f32[1,256,768]{2,1,0:T(8,128)}, f32[1,256,768]{2,1,0:T(8,128)}, f32[1,256,768]{2,1,0:T(8,128)}, ...) | async-done | bytes 4718608 | tf_op jit(solution)/shard_map/psum | solution.py:96
  1357.8 31.2 %all-reduce.6 = (f32[768]{0:T(1024)S(1)}, f32[32,3]{0,1:T(4,128)}, f32[768]{0:T(1024)S(1)}, f32[768]{0:T(1024)S(1)}) all-reduce(f32[768]{0:T(1024)S(1)} %add_add_fusion.14, f32[32,3]{0,1:T(4,128)S(1)} %copy-done.241, f32[768]{0:T(1024)S(1)} %copy-done.220, ...), channel_id=26, replica_groups=mesh['dp'=2,'ctx'=4,'tp'=4] {'dp','ctx'}, use_global_device_ids=true, to_apply=%region_69.70.clone | all-reduce | flops 2400 | bytes 19200
  1398.9 41.4 %reduce-scatter.68.cloned.1.call-done = f32[512,96]{0,1:T(8,128)} async-done(((f32[512,768]{0,1:T(8,128)}), f32[512,96]{0,1:T(8,128)}) %reduce-scatter.68.cloned.1.call-update) | async-done | bytes 196624 | tf_op jit(solution)/shard_map/reduce_scatter | solution.py:118
  1440.4 41.9 %reduce-scatter.64.cloned.1.call-done = f32[96,512]{1,0:T(8,128)} async-done(((f32[768,512]{1,0:T(8,128)}), f32[96,512]{1,0:T(8,128)}) %reduce-scatter.64.cloned.1.call-update) | async-done | bytes 196624 | tf_op jit(solution)/shard_map/reduce_scatter | solution.py:114
  1482.2 36.4 %reduce-scatter.62.cloned.1.call-done = f32[96,192]{1,0:T(8,128)} async-done(((f32[768,192]{1,0:T(8,128)}), f32[96,192]{1,0:T(8,128)}) %reduce-scatter.62.cloned.1.call-update) | async-done | bytes 73744 | tf_op jit(solution)/shard_map/reduce_scatter | solution.py:111
  1518.6 35.6 %reduce-scatter.74.cloned.1.call-done = f32[96,192]{1,0:T(8,128)} async-done(((f32[768,192]{1,0:T(8,128)}), f32[96,192]{1,0:T(8,128)}) %reduce-scatter.74.cloned.1.call-update) | async-done | bytes 73744
  1554.3 35.8 %reduce-scatter.72.cloned.1.call-done = f32[96,192]{1,0:T(8,128)} async-done(((f32[768,192]{1,0:T(8,128)}), f32[96,192]{1,0:T(8,128)}) %reduce-scatter.72.cloned.1.call-update) | async-done | bytes 73744
  1590.0 35.7 %reduce-scatter.56.cloned.1.call-done = f32[96,192]{1,0:T(8,128)} async-done(((f32[768,192]{1,0:T(8,128)}), f32[96,192]{1,0:T(8,128)}) %reduce-scatter.56.cloned.1.call-update) | async-done | bytes 73744 | tf_op jit(solution)/shard_map/reduce_scatter | solution.py:108
  1625.7 35.6 %reduce-scatter.60.cloned.1.call-done = f32[96,192]{1,0:T(8,128)} async-done(((f32[768,192]{1,0:T(8,128)}), f32[96,192]{1,0:T(8,128)}) %reduce-scatter.60.cloned.1.call-update) | async-done | bytes 73744 | tf_op jit(solution)/shard_map/reduce_scatter | solution.py:110
  1661.4 35.7 %reduce-scatter.58.cloned.1.call-done = f32[96,192]{1,0:T(8,128)} async-done(((f32[768,192]{1,0:T(8,128)}), f32[96,192]{1,0:T(8,128)}) %reduce-scatter.58.cloned.1.call-update) | async-done | bytes 73744 | tf_op jit(solution)/shard_map/reduce_scatter | solution.py:109
  (800 shorter events, 775.2 us)
Async XLA Ops:
  7.2 517.3 %all-reduce.27.cloned.1.call-start = ((), (), s32[]{:S(2)}) async-start(), calls=%async_computation.50 | async-start | bytes 4718592 | tf_op jit(solution)/shard_map/psum | solution.py:96
  317.1 315.6 %all-reduce.25.cloned.1.call-start = ((), (), s32[]{:S(2)}) async-start(), calls=%async_computation.49 | async-start | bytes 4718592 | tf_op jit(solution)/shard_map/psum | solution.py:96
  542.3 183.3 %all-reduce.23.cloned.1.call-start = ((), (), s32[]{:S(2)}) async-start(), calls=%async_computation.48 | async-start | bytes 4718592 | tf_op jit(solution)/shard_map/psum | solution.py:100
  650.2 129.1 %reduce-scatter.32.cloned.1.call-start = ((), (), s32[]{:S(2)}) async-start(), calls=%async_computation.23 | async-start | bytes 983040 | tf_op jit(solution)/shard_map/reduce_scatter | solution.py:266
  751.5 85.1 %reduce-scatter.42.cloned.1.call-start = ((), (), s32[]{:S(2)}) async-start(), calls=%async_computation.28 | async-start | bytes 983040 | tf_op jit(solution)/shard_map/reduce_scatter | solution.py:269
  755.4 106.3 %reduce-scatter.48.cloned.1.call-start = ((), (), s32[]{:S(2)}) async-start(), calls=%async_computation.31 | async-start | bytes 983040 | tf_op jit(solution)/shard_map/reduce_scatter | solution.py:266
  764.5 122.2 %reduce-scatter.50.cloned.1.call-start = ((), (), s32[]{:S(2)}) async-start(), calls=%async_computation.32 | async-start | bytes 983040 | tf_op jit(solution)/shard_map/reduce_scatter | solution.py:269
  774.6 229.2 %all-reduce.21.cloned.1.call-start = ((), (), s32[]{:S(2)}) async-start(), calls=%async_computation.47 | async-start | bytes 9437184 | tf_op jit(solution)/shard_map/psum | solution.py:100
  890.7 179.6 %reduce-scatter.36.cloned.1.call-start = ((), (), s32[]{:S(2)}) async-start(), calls=%async_computation.25 | async-start | bytes 983040 | tf_op jit(solution)/shard_map/reduce_scatter | solution.py:308
  1030.8 85.5 %reduce-scatter.46.cloned.1.call-start = ((), (), s32[]{:S(2)}) async-start(), calls=%async_computation.30 | async-start | bytes 983040 | tf_op jit(solution)/shard_map/reduce_scatter | solution.py:311
  1035.8 105.3 %reduce-scatter.52.cloned.1.call-start = ((), (), s32[]{:S(2)}) async-start(), calls=%async_computation.33 | async-start | bytes 983040 | tf_op jit(solution)/shard_map/reduce_scatter | solution.py:308
  1043.3 122.7 %reduce-scatter.54.cloned.1.call-start = ((), (), s32[]{:S(2)}) async-start(), calls=%async_computation.34 | async-start | bytes 983040 | tf_op jit(solution)/shard_map/reduce_scatter | solution.py:311
  1045.9 155.8 %reduce-scatter.76.cloned.1.call-start = ((), (), s32[]{:S(2)}) async-start(), calls=%async_computation.45 | async-start | bytes 884736
  1056.2 223.6 %reduce-scatter.70.cloned.1.call-start = ((), (), s32[]{:S(2)}) async-start(), calls=%async_computation.42 | async-start | bytes 884736
  1070.3 285.2 %all-reduce.19.cloned.1.call-start = ((), (), s32[]{:S(2)}) async-start(), calls=%async_computation.46 | async-start | bytes 9437184 | tf_op jit(solution)/shard_map/psum | solution.py:96
  1168.6 230.3 %reduce-scatter.66.cloned.1.call-start = ((), (), s32[]{:S(2)}) async-start(), calls=%async_computation.40 | async-start | bytes 1769472 | tf_op jit(solution)/shard_map/reduce_scatter | solution.py:115
  1173.2 267.1 %reduce-scatter.68.cloned.1.call-start = ((), (), s32[]{:S(2)}) async-start(), calls=%async_computation.41 | async-start | bytes 1769472 | tf_op jit(solution)/shard_map/reduce_scatter | solution.py:118
  1178.2 304.0 %reduce-scatter.64.cloned.1.call-start = ((), (), s32[]{:S(2)}) async-start(), calls=%async_computation.39 | async-start | bytes 1769472 | tf_op jit(solution)/shard_map/reduce_scatter | solution.py:114
  1182.9 335.7 %reduce-scatter.62.cloned.1.call-start = ((), (), s32[]{:S(2)}) async-start(), calls=%async_computation.38 | async-start | bytes 884736 | tf_op jit(solution)/shard_map/reduce_scatter | solution.py:111
  1187.5 366.7 %reduce-scatter.74.cloned.1.call-start = ((), (), s32[]{:S(2)}) async-start(), calls=%async_computation.44 | async-start | bytes 884736
  1194.6 395.4 %reduce-scatter.72.cloned.1.call-start = ((), (), s32[]{:S(2)}) async-start(), calls=%async_computation.43 | async-start | bytes 884736
  1210.5 415.3 %reduce-scatter.56.cloned.1.call-start = ((), (), s32[]{:S(2)}) async-start(), calls=%async_computation.35 | async-start | bytes 884736 | tf_op jit(solution)/shard_map/reduce_scatter | solution.py:108
  1252.6 408.8 %reduce-scatter.60.cloned.1.call-start = ((), (), s32[]{:S(2)}) async-start(), calls=%async_computation.37 | async-start | bytes 884736 | tf_op jit(solution)/shard_map/reduce_scatter | solution.py:110
  1276.3 420.8 %reduce-scatter.58.cloned.1.call-start = ((), (), s32[]{:S(2)}) async-start(), calls=%async_computation.36 | async-start | bytes 884736 | tf_op jit(solution)/shard_map/reduce_scatter | solution.py:109
  (246 other events, 3386.0 us)
Sparse Core Ops, SparseCore 0:
  317.2 74.7 all-reduce.26
  542.4 75.0 all-reduce.24
  650.3 75.2 all-reduce.22
  738.6 23.2 reduce-scatter.31
  764.2 22.5 reduce-scatter.33
  789.0 22.5 reduce-scatter.39
  814.0 22.6 reduce-scatter.41
  864.1 22.5 reduce-scatter.49
  891.3 112.4 all-reduce.20
  1018.3 23.3 reduce-scatter.35
  1068.9 22.5 reduce-scatter.43
  1143.4 22.5 reduce-scatter.53
  1168.2 33.4 reduce-scatter.75
  1203.9 32.7 reduce-scatter.69
  1242.2 113.1 all-reduce.18
  1358.3 40.6 reduce-scatter.65
  1401.9 38.3 reduce-scatter.67
  1443.3 38.8 reduce-scatter.63
  1485.2 33.3 reduce-scatter.61
  1521.3 32.8 reduce-scatter.73
  1557.2 32.7 reduce-scatter.71
  1592.8 32.9 reduce-scatter.55
  1628.5 32.7 reduce-scatter.59
  1664.2 32.7 reduce-scatter.57
  (4 shorter events, 89.9 us)
where the time goes:
time: 1710 us; the launch traced here: 1700 us
  waiting for transfers between devices  737 us (43%)
  blocking collectives  587 us (34%)
  matrix products  257 us (15%)
  other arithmetic  64.5 us (4%)
  local copies, waits for them, and re-layouts  36.6 us (2%)
  between operations  19.1 us (1%)
    psum x2, waiting for transfers between devices, input_sum(): return lax.psum(partial_rows, 'tp')  186 us
    unnamed x32, waiting for transfers between devices  78.3 us
    psum x3, waiting for transfers between devices, branch_sum(): return lax.psum(partial_rows, 'tp')  69.2 us
    dot_general x3, matrix products, per_device(): jnp.einsum('vcz,ecz->ev', jnp.sum(self_score_gradient, axis=0), bucket_in...  57.5 us
    dot_general x33, matrix products, project_back(): jnp.einsum('sth,dh->std', grad_rows, weight, preferred_element_type=jnp.f...  52.6 us
    reduce_scatter x3, waiting for transfers between devices, per_device(): lax.psum_scatter(d_cvalue.reshape(per_batch, enc_length, -1), 'ctx', scat...  50.7 us
    unnamed x2, blocking collectives  50.7 us
    all_gather x3, blocking collectives, per_device(): lax.all_gather(ckey_local, 'ctx', axis=1, tiled=True)  47.3 us
  transfers between devices with their start and end apart: 28, of which 22 were waited for; matrix products, arithmetic and copies ran while one was open for 14% of the time, Pallas kernels for 0%

commit v1 on v0

v1 whole, which is shorter than its diff:
```python
import jax
import jax.numpy as jnp
import numpy as np
from jax import lax
from jax.experimental import pallas as pl
from jax.experimental.pallas import tpu as pltpu
from jax.sharding import PartitionSpec as P

HEAD_DIM = 64
NB = 32
EPS = 1e-06
NEG = -1e30
BF = jnp.bfloat16
F32 = jnp.float32
FULL_PRECISION = lax.Precision.HIGHEST
bucket_edges = [int(np.ceil(16.0 * 8.0 ** (slot_index / 16.0))) for slot_index in range(1, 16)]
NN = (((1,), (0,)), ((), ()))
NT = (((1,), (1,)), ((), ()))
TN = (((0,), (0,)), ((), ()))
GELU_C = float(np.sqrt(2.0 / np.pi))


def bucket_index(distance):
    clipped = jnp.maximum(distance, 0)
    result = jnp.minimum(clipped, 16)
    for edge_value in bucket_edges:
        result = result + (clipped >= edge_value).astype(jnp.int32)
    return result


def mm(left, right, dims=NN):
    return lax.dot_general(left, right, dims, preferred_element_type=F32)


def run(name, body, scal, ins, outs, grid=1, scratch=(), flops=0):
    def spec(shape, kind):
        rest = (0,) * (len(shape) - 1)
        if kind == "s":
            return pl.BlockSpec((1,) + tuple(shape[1:]), lambda s, sc: (s,) + rest)
        if kind == "c":
            block = (shape[0], 1) + tuple(shape[2:])
            return pl.BlockSpec(block, lambda s, sc: (0, s) + (0,) * (len(shape) - 2))
        if isinstance(kind, int):
            return pl.BlockSpec((shape[0], kind, shape[2]), lambda s, sc: (0, sc[0], 0))
        return pl.BlockSpec(tuple(shape), lambda s, sc: (0,) + rest)

    n_in, n_out = len(ins), len(outs)

    def kernel(sc, *refs):
        body(sc, refs[:n_in], refs[n_in : n_in + n_out], refs[n_in + n_out :])

    moved = sum(int(np.prod(a.shape)) * a.dtype.itemsize for a, _ in ins)
    moved += sum(int(np.prod(s)) * jnp.dtype(d).itemsize for s, d, _ in outs)
    return pl.pallas_call(
        kernel,
        out_shape=[jax.ShapeDtypeStruct(tuple(s), d) for s, d, _ in outs],
        grid_spec=pltpu.PrefetchScalarGridSpec(
            num_scalar_prefetch=1,
            grid=(grid,),
            in_specs=[spec(a.shape, k) for a, k in ins],
            out_specs=[spec(s, k) for s, _, k in outs],
            scratch_shapes=list(scratch),
        ),
        compiler_params=pltpu.CompilerParams(dimension_semantics=("arbitrary",)),
        cost_estimate=pl.CostEstimate(flops=int(flops), bytes_accessed=moved, transcendentals=0),
        name=name,
    )(scal, *[a for a, _ in ins])


def rows_at(index, size):
    return pl.ds(pl.multiple_of(index * size, size), size)


def norm_fwd(v, gain):
    inv = lax.rsqrt(jnp.mean(v * v, axis=-1, keepdims=True) + EPS)
    return (v * inv * gain).astype(BF)


def norm_bwd(dy, v, gain):
    inv = lax.rsqrt(jnp.mean(v * v, axis=-1, keepdims=True) + EPS)
    unit = v * inv
    d_gain = jnp.sum(dy * unit, axis=0, keepdims=True)
    d_unit = dy * gain
    inner = jnp.mean(d_unit * unit, axis=-1, keepdims=True)
    return inv * (d_unit - unit * inner), d_gain


def put_pieces(sc, scratch, piece_refs, value):
    scratch[...] = value
    size = piece_refs[0].shape[1]
    for m, ref in enumerate(piece_refs):
        ref[0] = scratch[rows_at(sc[m], size), :].astype(ref.dtype)


def take_pieces(sc, scratch, piece_refs):
    size = piece_refs[0].shape[1]
    for m, ref in enumerate(piece_refs):
        scratch[rows_at(sc[m], size), :] = ref[0]


def head_lane(width):
    return lax.broadcasted_iota(jnp.int32, (1, width), 1) // HEAD_DIM


def only_head(value, lane, h):
    return jnp.where(lane == h, value, jnp.zeros_like(value))


def attend(q, k, v, p_ref, heads, bias_of, allowed):
    lane = head_lane(q.shape[1])
    out = jnp.zeros(q.shape, F32)
    for h in range(heads):
        scores = mm(only_head(q, lane, h), k, NT)
        if bias_of is not None:
            scores = scores + bias_of(h)
        scores = jnp.where(allowed, scores, NEG)
        top = jnp.max(scores, axis=-1, keepdims=True)
        e = jnp.exp(scores - top)
        prob = (e * (1.0 / jnp.sum(e, axis=-1, keepdims=True))).astype(BF)
        p_ref[0, h] = prob
        out = jnp.where(lane == h, mm(prob, v), out)
    return out


def attend_back(d_out, q, k, v, p_ref, heads, keep):
    lane = head_lane(q.shape[1])
    dq = jnp.zeros(q.shape, F32)
    dk = dv = None
    for h in range(heads):
        d_head = only_head(d_out, lane, h)
        low_p = p_ref[0, h]
        prob = low_p.astype(F32)
        d_prob = mm(d_head, v, NT)
        both = prob * d_prob
        d_score = both - prob * jnp.sum(both, axis=-1, keepdims=True)
        if keep is not None:
            keep(h, d_score)
        low = d_score.astype(BF)
        dq = jnp.where(lane == h, mm(low, k), dq)
        dk_h = mm(low, only_head(q, lane, h), TN)
        dv_h = mm(low_p, d_head, TN)
        dk = dk_h if dk is None else dk + dk_h
        dv = dv_h if dv is None else dv + dv_h
    return dq, dk, dv


def per_device(
    inputs,
    encoder_out,
    segments,
    encoder_segments,
    self_gain,
    w_query,
    w_key,
    w_value,
    w_out,
    relative_bucket_bias,
    cross_gain,
    cw_query,
    cw_key,
    cw_value,
    cw_out,
    ff_gain,
    w_gate,
    w_up,
    w_down,
    cotangent,
):
    C, TP, DP = lax.axis_size("ctx"), lax.axis_size("tp"), lax.axis_size("dp")
    c, t, d = lax.axis_index("ctx"), lax.axis_index("tp"), lax.axis_index("dp")
    S, NR, D = inputs.shape
    ER = encoder_out.shape[1]
    HD = w_query.shape[1]
    HH = HD // HEAD_DIM
    FF = w_gate.shape[1]
    QR, QE = NR // TP, ER // TP
    RQ = S * QR
    L, E = NR * C, ER * C
    G = w_query.shape[0]
    DH = D // DP
    H = min(C - 1, -(-(L // 2 - 1) // NR))
    W = (H + 1) * NR
    N = -(-(NR + W) // 128) * 128
    near = C <= 4
    scal = jnp.stack([t ^ m for m in range(TP)] + [d, (d + 1) % DP] + [(c + m) % C for m in range(min(C, 4))])
    scal = scal.astype(jnp.int32)
    I_DP, I_CTX = TP, TP + 2

    def tp_swap(x, m):
        return lax.ppermute(x, "tp", [(i, i ^ m) for i in range(TP)])

    def dp_swap(x):
        return lax.ppermute(x, "dp", [(i, (i + 1) % DP) for i in range(DP)])

    def ctx_from(x, m):
        return lax.ppermute(x, "ctx", [((i + m) % C, i) for i in range(C)])

    def ctx_to(x, m):
        return lax.ppermute(x, "ctx", [(i, (i + m) % C) for i in range(C)])

    def ctx_up(x, k):
        return lax.ppermute(x, "ctx", [(i, i + k) for i in range(C - k)])

    def ctx_down(x, k):
        return lax.ppermute(x, "ctx", [(i + k, i) for i in range(C - k)])

    def tp_gather(x):
        return [x] + [tp_swap(x, m) for m in range(1, TP)]

    def tp_exchange(pieces):
        return [pieces[0]] + [tp_swap(pieces[m], m) for m in range(1, TP)]

    gains_here = jnp.stack([self_gain, cross_gain, ff_gain]).astype(F32)
    if near:
        small = jnp.concatenate(
            [
                segments.astype(F32).reshape(-1),
                encoder_segments.astype(F32).reshape(-1),
                gains_here.reshape(-1),
            ]
        )[None]
        smalls = [small] + [ctx_from(small, m) for m in range(1, C)]
        n_seg, n_eseg = S * NR, S * ER
        segs = [v[0, :n_seg].reshape(S, NR) for v in smalls]
        esegs = [v[0, n_seg : n_seg + n_eseg].reshape(S, ER) for v in smalls]
        seg_keys = jnp.concatenate(
            [jnp.where(c >= k, segs[C - k], -1.0) for k in range(H, 0, -1)] + [segs[0]], axis=1
        )
        eseg_keys = jnp.concatenate(esegs, axis=1)
        turned = jnp.stack([v[0, n_seg + n_eseg :].reshape(3, G) for v in smalls], axis=1)
        turned = lax.dynamic_slice_in_dim(jnp.concatenate([turned, turned], axis=1), (C - c) % C, C, 1)
        turned = turned.reshape(3, C * G)
        other = dp_swap(turned)
        gains = jnp.where(
            d == 0, jnp.concatenate([turned, other], axis=1), jnp.concatenate([other, turned], axis=1)
        )
    else:
        seg_all = lax.all_gather(segments.astype(F32), "ctx", axis=1, tiled=True)
        seg_all = jnp.concatenate([jnp.full((S, H * NR), -1.0, F32), seg_all], axis=1)
        seg_keys = lax.dynamic_slice_in_dim(seg_all, c * NR, W, 1)
        eseg_keys = lax.all_gather(encoder_segments.astype(F32), "ctx", axis=1, tiled=True)
        gains = lax.all_gather(gains_here, ("dp", "ctx"), axis=1, tiled=True)
    gain_one, gain_two, gain_three = gains[0:1], gains[1:2], gains[2:3]
    seg_rows = segments.astype(F32).reshape(S, NR, 1)
    seg_keys = seg_keys.reshape(S, 1, W)
    eseg_keys = eseg_keys.reshape(S, 1, E)

    pack_one = jnp.concatenate([w_query, w_key, w_value], axis=1)
    pack_two = jnp.concatenate([w_out.T, cw_query, cw_out.T], axis=1)
    pack_kv = jnp.concatenate([cw_key, cw_value], axis=1)
    pack_ff = jnp.concatenate([w_gate, w_up, w_down.T], axis=1)

    def whole_rows(packed, widths):
        if not near:
            full = lax.all_gather(packed, ("dp", "ctx"), axis=0, tiled=True)
            edges = np.cumsum([0] + list(widths))
            return [full[:, a:b] for a, b in zip(edges[:-1], edges[1:])]
        own = [packed] + [ctx_from(packed, m) for m in range(1, C)]
        other = [dp_swap(v) for v in own]

        def body(sc, ins, outs, scratch):
            for j in range(2):
                for m in range(C):
                    block = ins[j * C + m]
                    at = pl.multiple_of(sc[I_DP + j] * DH + sc[I_CTX + m] * G, 16)
                    first = 0
                    for ref, width in zip(outs, widths):
                        ref[pl.ds(at, G), :] = block[:, first : first + width]
                        first += width

        return run(
            "weight_rows",
            body,
            scal,
            [(v, None) for v in own + other],
            [((D, width), BF, None) for width in widths],
        )

    wq, wk, wv = whole_rows(pack_one, (HD, HD, HD))

    def every_rank(packed, count):
        if not near:
            full = lax.all_gather(packed, ("dp", "ctx"), axis=0, tiled=True)
            return [[v[:, i * HD : (i + 1) * HD] for i in range(count)] for v in tp_gather(full)]
        own = [packed] + [ctx_from(packed, m) for m in range(1, C)]
        width = packed.shape[1]

        def half_body(sc, ins, outs, scratch):
            for m in range(C):
                outs[0][pl.ds(pl.multiple_of(sc[I_CTX + m] * G, 16), G), :] = ins[m][...]

        (half,) = run("half_rows", half_body, scal, [(v, None) for v in own], [((DH, width), BF, None)])
        halves = tp_gather(half)
        others = [dp_swap(v) for v in halves]

        def body(sc, ins, outs, scratch):
            for j in range(2):
                for m in range(TP):
                    at = rows_at(sc[I_DP + j], DH)
                    for i in range(count):
                        outs[m * count + i][at, :] = ins[j * TP + m][:, i * HD : (i + 1) * HD]

        flat = run(
            "rank_rows",
            body,
            scal,
            [(v, None) for v in halves + others],
            [((D, HD), BF, None)] * (TP * count),
        )
        return [flat[m * count : (m + 1) * count] for m in range(TP)]

    def pre_body(sc, ins, outs, scratch):
        outs[0][0] = norm_fwd(ins[0][0], ins[1][...])
        outs[1][0] = outs[0][0, rows_at(sc[0], QR), :]

    act_one, act_quarter = run(
        "act_one",
        pre_body,
        scal,
        [(inputs, "s"), (gain_one, None)],
        [((S, NR, D), BF, "s"), ((S, QR, D), BF, "s")],
        grid=S,
    )
    if near:
        halo, halo_at = [], []
        for k in range(1, H + 1):
            for m, piece in enumerate(tp_gather(ctx_up(act_quarter, k))):
                halo.append(piece)
                halo_at.append(((H - k) * NR, m))
    else:
        act_all = lax.all_gather(act_one, "ctx", axis=1, tiled=True)
        act_all = jnp.concatenate([jnp.zeros((S, H * NR, D), BF), act_all], axis=1)
        halo = [lax.dynamic_slice_in_dim(act_all, c * NR, H * NR, 1)]
        halo_at = [(0, None)]

    row_of = jnp.arange(N, dtype=jnp.int32)
    lane_distance = jnp.where(row_of < W, H * NR - row_of, H * NR + N - row_of)
    bucket_here = (bucket_index(lane_distance)[None] == jnp.arange(NB, dtype=jnp.int32)[:, None]).astype(F32)
    bias_lanes = jnp.einsum("bh,bn->hn", relative_bucket_bias, bucket_here, precision=FULL_PRECISION)

    n_halo = len(halo)

    def self_body(sc, ins, outs, scratch):
        act, parts = ins[0], ins[1 : 1 + n_halo]
        rq, rk, rv, seg_q, seg_k, lanes = ins[1 + n_halo :]
        q_ref, k_ref, v_ref, p_ref = outs[:4]
        window, bias, att = scratch

        @pl.when(pl.program_id(0) == 0)
        def _():
            for h in range(HH):
                line = jnp.broadcast_to(lanes[h : h + 1, :], (NR, N))
                bias[h] = pltpu.roll(line, 0, 1, stride=1, stride_axis=0)[:, :W]

        for part, (base, m) in zip(parts, halo_at):
            if m is None:
                window[base : base + part.shape[1], :] = part[0]
            else:
                at = pl.multiple_of(base + sc[m] * QR, 16)
                window[pl.ds(at, QR), :] = part[0]
        window[H * NR :, :] = act[0]
        q = mm(act[0], rq[...]).astype(BF)
        k = mm(window[...], rk[...]).astype(BF)
        v = mm(window[...], rv[...]).astype(BF)
        q_ref[0], k_ref[0], v_ref[0] = q, k, v
        ahead = lax.broadcasted_iota(jnp.int32, (NR, W), 1) - lax.broadcasted_iota(jnp.int32, (NR, W), 0)
        allowed = (ahead <= H * NR) & (seg_q[0] == seg_k[0])
        out = attend(q, k, v, p_ref, HH, lambda h: bias[h], allowed)
        put_pieces(sc, att, outs[4:], out)

    self_out = run(
        "self_attention",
        self_body,
        scal,
        [(act_one, "s")]
        + [(v, "s") for v in halo]
        + [(wq, None), (wk, None), (wv, None), (seg_rows, "s"), (seg_keys, "s"), (bias_lanes, None)],
        [((S, NR, HD), BF, "s"), ((S, W, HD), BF, "s"), ((S, W, HD), BF, "s"), ((S, HH, NR, W), BF, "s")]
        + [((S, QR, HD), BF, "s")] * TP,
        grid=S,
        scratch=[pltpu.VMEM((W, D), BF), pltpu.VMEM((HH, NR, W), F32), pltpu.VMEM((NR, HD), F32)],
        flops=2 * S * (NR * D * HD + 2 * W * D * HD + 2 * HH * NR * W * HD),
    )
    q_self, k_self, v_self, p_self = self_out[:4]
    att_ranks = [v.reshape(RQ, HD) for v in tp_exchange(self_out[4:])]

    ranks = every_rank(pack_two, 3)
    wo_ranks, cwq_ranks, co_ranks = [[r[i] for r in ranks] for i in range(3)]

    def out_body(sc, ins, outs, scratch):
        x = ins[0][...].reshape(RQ, D)
        parts, weights = ins[1 : 1 + TP], ins[1 + TP : 1 + 2 * TP]
        queries, gain = ins[1 + 2 * TP : 1 + 3 * TP], ins[-1]
        resid = x
        for part, weight in zip(parts, weights):
            resid = resid + mm(part[...], weight[...], NT)
        act = norm_fwd(resid, gain[...])
        outs[0][...], outs[1][...] = resid, act
        for ref, weight in zip(outs[2:], queries):
            ref[...] = mm(act, weight[...]).astype(BF)

    out_res = run(
        "self_out",
        out_body,
        scal,
        [(inputs, QR)] + [(v, None) for v in att_ranks + wo_ranks + cwq_ranks + [gain_two]],
        [((RQ, D), F32, None), ((RQ, D), BF, None)] + [((RQ, HD), BF, None)] * TP,
        flops=4 * RQ * D * HD * TP,
    )
    resid_one, act_two = out_res[:2]
    cq_parts = [v.reshape(S, QR, HD) for v in tp_exchange(out_res[2:])]

    cwk, cwv = whole_rows(pack_kv, (HD, HD))
    if near:
        enc_quarter = lax.dynamic_slice_in_dim(encoder_out, t * QE, QE, 1)
        far = jnp.stack([ctx_from(enc_quarter, m) for m in range(1, C)])
        enc_parts = [(v, "c") for v in tp_gather(far)]
    else:
        enc_parts = [(lax.all_gather(encoder_out, "ctx", axis=1, tiled=True), "s")]

    def ckv_body(sc, ins, outs, scratch):
        own, parts = ins[0], ins[1 : 1 + len(enc_parts)]
        rk, rv = ins[1 + len(enc_parts) :]
        window = scratch[0]
        if near:
            window[:ER, :] = own[0]
            for m in range(1, C):
                for n in range(TP):
                    at = pl.multiple_of(m * ER + sc[n] * QE, 16)
                    window[pl.ds(at, QE), :] = parts[n][m - 1, 0]
        else:
            window[...] = parts[0][0]
        outs[0][0] = mm(window[...], rk[...]).astype(BF)
        outs[1][0] = mm(window[...], rv[...]).astype(BF)

    k_cross, v_cross = run(
        "cross_keys",
        ckv_body,
        scal,
        [(encoder_out, "s")] + enc_parts + [(cwk, None), (cwv, None)],
        [((S, E, HD), BF, "s")] * 2,
        grid=S,
        scratch=[pltpu.VMEM((E, D), BF)],
        flops=4 * S * E * D * HD,
    )

    def cross_body(sc, ins, outs, scratch):
        k_ref, v_ref, seg_q, seg_k = ins[TP:]
        cq_ref, p_ref = outs[:2]
        cq, att = scratch
        take_pieces(sc, cq, ins[:TP])
        q = cq[...]
        cq_ref[0] = q
        allowed = seg_q[0] == seg_k[0]
        out = attend(q, k_ref[0], v_ref[0], p_ref, HH, None, allowed)
        put_pieces(sc, att, outs[2:], out)

    cross_out = run(
        "cross_attention",
        cross_body,
        scal,
        [(v, "s") for v in cq_parts] + [(k_cross, "s"), (v_cross, "s"), (seg_rows, "s"), (eseg_keys, "s")],
        [((S, NR, HD), BF, "s"), ((S, HH, NR, E), BF, "s")] + [((S, QR, HD), BF, "s")] * TP,
        grid=S,
        scratch=[pltpu.VMEM((NR, HD), BF), pltpu.VMEM((NR, HD), F32)],
        flops=4 * S * HH * NR * E * HD,
    )
    q_cross, p_cross = cross_out[:2]
    catt_ranks = [v.reshape(RQ, HD) for v in tp_exchange(cross_out[2:])]

    def cout_body(sc, ins, outs, scratch):
        resid = ins[0][...]
        for part, weight in zip(ins[1 : 1 + TP], ins[1 + TP : 1 + 2 * TP]):
            resid = resid + mm(part[...], weight[...], NT)
        outs[0][...] = resid
        outs[1][...] = norm_fwd(resid, ins[-1][...])

    resid_two, act_three_q = run(
        "cross_out",
        cout_body,
        scal,
        [(v, None) for v in [resid_one] + catt_ranks + co_ranks + [gain_three]],
        [((RQ, D), F32, None), ((RQ, D), BF, None)],
        flops=2 * RQ * D * HD * TP,
    )
    act_three_parts = tp_gather(act_three_q.reshape(S, QR, D))

    wg, wu, wd = whole_rows(pack_ff, (FF, FF, FF))

    def ffn_body(sc, ins, outs, scratch):
        cot, rg, ru, rd = ins[TP:]
        act_ref, hid_ref, dgu_ref = outs[:3]
        rows, total = scratch
        take_pieces(sc, rows, ins[:TP])
        act = rows[...]
        act_ref[0] = act
        gate = mm(act, rg[...])
        up = mm(act, ru[...])
        inside = jnp.tanh(GELU_C * (gate + 0.044715 * gate * gate * gate))
        half = 0.5 * (1.0 + inside)
        gelu = gate * half
        slope = half + 0.5 * gate * (1.0 - inside * inside) * (GELU_C * (1.0 + 3 * 0.044715 * gate * gate))
        hidden = (gelu * up).astype(BF)
        hid_ref[0] = hidden
        put_pieces(sc, total, outs[3 : 3 + TP], mm(hidden, rd[...], NT))
        d_hidden = mm(cot[0].astype(BF), rd[...])
        d_gate = (d_hidden * up * slope).astype(BF)
        d_up = (d_hidden * gelu).astype(BF)
        dgu_ref[0, :, :FF] = d_gate
        dgu_ref[0, :, FF:] = d_up
        put_pieces(sc, total, outs[3 + TP :], mm(d_gate, rg[...], NT) + mm(d_up, ru[...], NT))

    piece_outs = [((S, QR, D), F32, "s")] + [((S, QR, D), BF, "s")] * (TP - 1)
    ffn_out = run(
        "feed_forward",
        ffn_body,
        scal,
        [(v, "s") for v in act_three_parts] + [(cotangent, "s"), (wg, None), (wu, None), (wd, None)],
        [((S, NR, D), BF, "s"), ((S, NR, FF), BF, "s"), ((S, NR, 2 * FF), BF, "s")] + piece_outs * 2,
        grid=S,
        scratch=[pltpu.VMEM((NR, D), BF), pltpu.VMEM((NR, D), F32)],
        flops=12 * S * NR * D * FF,
    )
    act_three, hidden, d_gate_up = ffn_out[:3]
    d_act_three = [v.reshape(RQ, D) for v in tp_exchange(ffn_out[3 + TP :])]

    def mid_three_body(sc, ins, outs, scratch):
        dy = ins[0][...]
        for part in ins[1:TP]:
            dy = dy + part[...]
        resid, cot, gain = ins[TP][...], ins[TP + 1][...].reshape(RQ, D), ins[TP + 2][...]
        dv, d_gain = norm_bwd(dy, resid, gain)
        grad = cot + dv
        low = grad.astype(BF)
        outs[0][...], outs[1][...], outs[2][...] = grad, low, d_gain
        for ref, weight in zip(outs[3:], ins[TP + 3 :]):
            ref[...] = mm(low, weight[...]).astype(BF)

    mid_three = run(
        "grad_two",
        mid_three_body,
        scal,
        [(v, None) for v in d_act_three]
        + [(resid_two, None), (cotangent, QR), (gain_three, None)]
        + [(v, None) for v in co_ranks],
        [((RQ, D), F32, None), ((RQ, D), BF, None), ((1, D), F32, None)] + [((RQ, HD), BF, None)] * TP,
        flops=2 * RQ * D * HD * TP,
    )
    grad_two, g_cross, d_ff_gain = mid_three[:3]
    d_catt_parts = [v.reshape(S, QR, HD) for v in tp_exchange(mid_three[3:])]

    def cross_back_body(sc, ins, outs, scratch):
        p_ref, q_ref, k_ref, v_ref = ins[TP:]
        d_rows, dq_rows = scratch
        take_pieces(sc, d_rows, ins[:TP])
        dq, dk, dv = attend_back(d_rows[...], q_ref[0], k_ref[0], v_ref[0], p_ref, HH, None)
        put_pieces(sc, dq_rows, outs[:TP], dq)
        size = outs[TP].shape[1]
        for m, ref in enumerate(outs[TP:]):
            ref[0, :, :HD] = dk[m * size : (m + 1) * size].astype(ref.dtype)
            ref[0, :, HD:] = dv[m * size : (m + 1) * size].astype(ref.dtype)

    if near:
        dckv_outs = [((S, ER, 2 * HD), F32, "s")] + [((S, ER, 2 * HD), BF, "s")] * (C - 1)
    else:
        dckv_outs = [((S, E, 2 * HD), BF, "s")]
    cross_back = run(
        "cross_backward",
        cross_back_body,
        scal,
        [(v, "s") for v in d_catt_parts] + [(p_cross, "s"), (q_cross, "s"), (k_cross, "s"), (v_cross, "s")],
        [((S, QR, HD), BF, "s")] * TP + dckv_outs,
        grid=S,
        scratch=[pltpu.VMEM((NR, HD), BF), pltpu.VMEM((NR, HD), F32)],
        flops=8 * S * HH * NR * E * HD,
    )
    d_cq_ranks = [v.reshape(RQ, HD) for v in tp_exchange(cross_back[:TP])]

    def mid_two_body(sc, ins, outs, scratch):
        parts, queries = ins[:TP], ins[TP : 2 * TP]
        resid, before, gain = ins[2 * TP][...], ins[2 * TP + 1][...], ins[2 * TP + 2][...]
        dy = mm(parts[0][...], queries[0][...], NT)
        for part, weight in zip(parts[1:], queries[1:]):
            dy = dy + mm(part[...], weight[...], NT)
        dv, d_gain = norm_bwd(dy, resid, gain)
        grad = before + dv
        low = grad.astype(BF)
        outs[0][...], outs[1][...], outs[2][...] = grad, low, d_gain
        for ref, weight in zip(outs[3:], ins[2 * TP + 3 :]):
            ref[...] = mm(low, weight[...]).astype(BF)

    mid_two = run(
        "grad_one",
        mid_two_body,
        scal,
        [(v, None) for v in d_cq_ranks + cwq_ranks + [resid_one, grad_two, gain_two] + wo_ranks],
        [((RQ, D), F32, None), ((RQ, D), BF, None), ((1, D), F32, None)] + [((RQ, HD), BF, None)] * TP,
        flops=4 * RQ * D * HD * TP,
    )
    grad_one, g_self, d_cross_gain = mid_two[:3]
    d_att_parts = [v.reshape(S, QR, HD) for v in tp_exchange(mid_two[3:])]

    def self_back_body(sc, ins, outs, scratch):
        p_ref, q_ref, k_ref, v_ref = ins[TP:]
        d_rows, shifted = scratch

        @pl.when(pl.program_id(0) == 0)
        def _():
            shifted[...] = jnp.zeros_like(shifted)

        def keep(h, d_score):
            shifted[h, :, :W] += d_score

        take_pieces(sc, d_rows, ins[:TP])
        dq, dk, dv = attend_back(d_rows[...], q_ref[0], k_ref[0], v_ref[0], p_ref, HH, keep)
        outs[0][0] = dq.astype(BF)
        size = outs[2].shape[1]
        outs[1][0, :, :HD], outs[1][0, :, HD:] = dk[H * NR :], dv[H * NR :]
        for n, ref in enumerate(outs[2:-1]):
            ref[0, :, :HD] = dk[n * size : (n + 1) * size].astype(BF)
            ref[0, :, HD:] = dv[n * size : (n + 1) * size].astype(BF)

        @pl.when(pl.program_id(0) == S - 1)
        def _():
            for h in range(HH):
                rows, block = NR, shifted[h]
                while rows > 1:
                    rows //= 2
                    block = block[:rows] + pltpu.roll(block[rows:], N - rows, 1)
                outs[-1][h : h + 1, :] = block

    halo_outs = [((S, NR, 2 * HD), BF, "s")] * H if near else [((S, H * NR, 2 * HD), BF, "s")]
    self_back = run(
        "self_backward",
        self_back_body,
        scal,
        [(v, "s") for v in d_att_parts] + [(p_self, "s"), (q_self, "s"), (k_self, "s"), (v_self, "s")],
        [((S, NR, HD), BF, "s"), ((S, NR, 2 * HD), F32, "s")] + halo_outs + [((HH, N), F32, None)],
        grid=S,
        scratch=[pltpu.VMEM((NR, HD), BF), pltpu.VMEM((HH, NR, N), F32)],
        flops=8 * S * HH * NR * W * HD,
    )
    dq_low, dkv_own, d_lanes = self_back[0], self_back[1], self_back[-1]
    if near:
        dkv_parts = [dkv_own] + [ctx_down(self_back[2 + H - k], k) for k in range(1, H + 1)]
    else:
        window = jnp.concatenate([self_back[2], dkv_own.astype(BF)], axis=1)
        spread = jnp.zeros((S, (H + C) * NR, 2 * HD), BF)
        spread = lax.dynamic_update_slice_in_dim(spread, window, c * NR, 1)
        dkv_parts = [
            lax.psum_scatter(spread[:, H * NR :], "ctx", scatter_dimension=1, tiled=True).astype(F32)
        ]

    def act_back_body(sc, ins, outs, scratch):
        total = ins[1][0]
        for part in ins[2:-3]:
            total = total + part[0]
        low = total.astype(BF)
        outs[0][0] = low
        rq, rk, rv = ins[-3:]
        grad = mm(ins[0][0], rq[...], NT) + mm(low[:, :HD], rk[...], NT) + mm(low[:, HD:], rv[...], NT)
        put_pieces(sc, scratch[0], outs[1:], grad)

    act_back = run(
        "self_projections_back",
        act_back_body,
        scal,
        [(dq_low, "s")] + [(v, "s") for v in dkv_parts] + [(wq, None), (wk, None), (wv, None)],
        [((S, NR, 2 * HD), BF, "s")] + piece_outs,
        grid=S,
        scratch=[pltpu.VMEM((NR, D), F32)],
        flops=6 * S * NR * D * HD,
    )
    dkv_low = act_back[0]
    d_act_one = [v.reshape(RQ, D) for v in tp_exchange(act_back[1:])]

    def last_body(sc, ins, outs, scratch):
        dy = ins[0][...]
        for part in ins[1:TP]:
            dy = dy + part[...]
        dv, d_gain = norm_bwd(dy, ins[TP][...].reshape(RQ, D), ins[TP + 1][...])
        outs[0][...] = (ins[TP + 2][...] + dv).astype(BF)
        outs[1][...] = d_gain

    d_in_quarter, d_self_gain = run(
        "d_inputs_rows",
        last_body,
        scal,
        [(v, None) for v in d_act_one] + [(inputs, QR), (gain_one, None), (grad_one, None)],
        [((RQ, D), BF, None), ((1, D), F32, None)],
    )

    def spread_rows(quarter, size):
        parts = tp_gather(quarter.reshape(S, size, D))

        def body(sc, ins, outs, scratch):
            for m, ref in enumerate(ins):
                outs[0][0, rows_at(sc[m], size), :] = ref[0].astype(F32)

        return run("all_rows", body, scal, [(v, "s") for v in parts], [((S, size * TP, D), F32, "s")], grid=S)[0]

    def sum_body(sc, ins, outs, scratch):
        total = ins[0][...]
        for ref in ins[1:]:
            total = total + ref[...]
        outs[0][...] = total.astype(BF)

    out_parts = [v.reshape(RQ, D) for v in tp_exchange(ffn_out[3 : 3 + TP])]
    (out_quarter,) = run(
        "output_rows", sum_body, scal, [(v, None) for v in [resid_two] + out_parts], [((RQ, D), BF, None)]
    )
    outputs = spread_rows(out_quarter, QR)

    if near:
        dckv_parts = [cross_back[TP]] + [ctx_to(cross_back[TP + m], m) for m in range(1, C)]
    else:
        dckv_parts = [lax.psum_scatter(cross_back[TP], "ctx", scatter_dimension=1, tiled=True).astype(F32)]

    def enc_back_body(sc, ins, outs, scratch):
        total = ins[0][0]
        for part in ins[1:-2]:
            total = total + part[0]
        low = total.astype(BF)
        outs[0][0] = low
        rk, rv = ins[-2:]
        put_pieces(sc, scratch[0], outs[1:], mm(low[:, :HD], rk[...], NT) + mm(low[:, HD:], rv[...], NT))

    enc_back = run(
        "encoder_back",
        enc_back_body,
        scal,
        [(v, "s") for v in dckv_parts] + [(cwk, None), (cwv, None)],
        [((S, ER, 2 * HD), BF, "s"), ((S, QE, D), F32, "s")] + [((S, QE, D), BF, "s")] * (TP - 1),
        grid=S,
        scratch=[pltpu.VMEM((ER, D), F32)],
        flops=4 * S * ER * D * HD,
    )
    dckv_low = enc_back[0]
    enc_sum = [v.reshape(S * QE, D) for v in tp_exchange(enc_back[1:])]
    (d_enc_quarter,) = run(
        "encoder_rows", sum_body, scal, [(v, None) for v in enc_sum], [((S * QE, D), BF, None)]
    )
    d_encoded = spread_rows(d_enc_quarter, QE)
    d_inputs = spread_rows(d_in_quarter, QR)

    def over_tokens(left, right):
        left, right = left.reshape(-1, left.shape[-1]), right.reshape(-1, right.shape[-1])
        return mm(left, right, TN)

    def core_half(full):
        if not near:
            return full
        other = lax.dynamic_slice_in_dim(full, ((d + 1) % DP) * DH, DH, 0).astype(BF)
        return lax.dynamic_slice_in_dim(full, d * DH, DH, 0) + dp_swap(other)

    def owners(rows):
        if not near:
            return lax.psum_scatter(rows.astype(BF), ("dp", "ctx"), scatter_dimension=0, tiled=True).astype(F32)
        total = lax.dynamic_slice_in_dim(rows, c * G, G, 0)
        for m in range(1, C):
            piece = lax.dynamic_slice_in_dim(rows, ((c + m) % C) * G, G, 0).astype(BF)
            total = total + ctx_to(piece, m)
        return total

    dw_ff = owners(
        core_half(
            jnp.concatenate(
                [over_tokens(act_three, d_gate_up), over_tokens(cotangent.astype(BF), hidden)], axis=1
            )
        )
    )
    rank_grads = []
    for left, rights in ((g_self, att_ranks), (act_two, d_cq_ranks), (g_cross, catt_ranks)):
        rank_grads.append(core_half(over_tokens(left, jnp.concatenate(rights, axis=1))))
    pieces = [
        jnp.concatenate([v[:, m * HD : (m + 1) * HD] for v in rank_grads], axis=1) for m in range(TP)
    ]
    dw_ranks = pieces[0]
    for m in range(1, TP):
        dw_ranks = dw_ranks + tp_swap(pieces[m].astype(BF), m)
    dw_here = core_half(
        jnp.concatenate(
            [
                over_tokens(act_one, dq_low),
                over_tokens(act_one, dkv_low),
                over_tokens(encoder_out, dckv_low),
            ],
            axis=1,
        )
    )
    dw_attn = owners(jnp.concatenate([dw_ranks, dw_here], axis=1))
    d_wo, d_cwq, d_co, d_wq, d_wk, d_wv, d_cwk, d_cwv = [
        dw_attn[:, i * HD : (i + 1) * HD] for i in range(8)
    ]
    d_wg, d_wu, d_wd = [dw_ff[:, i * FF : (i + 1) * FF] for i in range(3)]

    gain_rows = jnp.concatenate([d_self_gain, d_cross_gain, d_ff_gain], axis=0)
    d_bias = jnp.einsum("hn,bn->bh", d_lanes, bucket_here, precision=FULL_PRECISION)
    if near:
        for m in (1, 2):
            if m < TP:
                gain_rows = gain_rows + tp_swap(gain_rows, m)
        flat = jnp.concatenate([gain_rows.reshape(-1), d_bias.reshape(-1)])[None]
        flat = flat + dp_swap(flat)
        for m in (1, 2):
            if m < C:
                flat = flat + lax.ppermute(flat, "ctx", [(i, i ^ m) for i in range(C)])
        gain_rows = flat[0, : 3 * D].reshape(3, D)
        d_bias = flat[0, 3 * D :].reshape(NB, HH)
    else:
        gain_rows = lax.psum(gain_rows, ("dp", "ctx", "tp"))
        d_bias = lax.psum(d_bias, ("dp", "ctx"))
    gain_rows = lax.dynamic_slice_in_dim(gain_rows, (d * C + c) * G, G, 1)

    return (
        outputs,
        d_inputs,
        d_encoded,
        gain_rows[0],
        d_wq,
        d_wk,
        d_wv,
        d_wo.T,
        d_bias,
        gain_rows[1],
        d_cwq,
        d_cwk,
        d_cwv,
        d_co.T,
        gain_rows[2],
        d_wg,
        d_wu,
        d_wd.T,
    )


def solution(mesh):
    rows, where = P("dp", "ctx", None), P("dp", "ctx")
    vec, tall, wide, buckets = P(("dp", "ctx")), P(("dp", "ctx"), "tp"), P("tp", ("dp", "ctx")), P(None, "tp")
    return jax.shard_map(
        per_device,
        mesh=mesh,
        in_specs=(
            (rows, rows, where, where, vec, tall, tall, tall, wide, buckets, vec, tall, tall, tall, wide, vec)
            + (tall, tall, wide, rows)
        ),
        out_specs=(
            (rows, rows, rows, vec, tall, tall, tall, wide, buckets, vec, tall, tall, tall, wide, vec)
            + (tall, tall, wide)
        ),
        check_vma=False,
    )
```

time: 1710 us -> 536 us (0.31)
  blocking collectives: 587 us -> 0 us
  waiting for transfers between devices: 737 us -> 153 us
  matrix products: 257 us -> 17.6 us
  starting transfers between devices: 2.18 us -> 155 us
  Pallas kernels: 0 us -> 133 us
  other arithmetic: 64.5 us -> 28.4 us
    all_gather x29 -> x0, blocking collectives: 537 us -> none  [the longest x3 47.3 us: per_device(): lax.all_gather(ckey_local, 'ctx', axis=1, tiled=True)]
    reduce_scatter x19 -> x0, waiting for transfers between devices: 403 us -> none  [the longest x3 50.7 us: per_device(): lax.psum_scatter(d_cvalue.reshape(per_batch, enc_length, -1), 'ctx', scat...]
    psum x5 -> x0, waiting for transfers between devices: 256 us -> none  [the longest x2 186 us: input_sum(): return lax.psum(partial_rows, 'tp')]
    dot_general x139 -> x10, matrix products: 257 us -> 17.6 us  [the longest x8 15.9 us: mm(): return lax.dot_general(left, right, dims, preferred_element_type=F32)]
    ppermute x0 -> x115, starting transfers between devices: none -> 155 us  [the longest x59 74.1 us: tp_swap(): return lax.ppermute(x, 'tp', [(i, i ^ m) for i in range(TP)])]
    ppermute x0 -> x115, waiting for transfers between devices: none -> 153 us  [the longest x59 62.7 us: tp_swap(): return lax.ppermute(x, 'tp', [(i, i ^ m) for i in range(TP)])]
    pallas_call x0 -> x24, Pallas kernels: none -> 133 us  [run(): pl.pallas_call(kernel, out_shape=[jax.ShapeDtypeStruct(tuple(s), d) for s...]
    unnamed x32 -> x0, waiting for transfers between devices: 78.3 us -> none
  transfers between devices with their start and end apart: 28 -> 115, of which waited for: 22 -> 34; matrix products, arithmetic and copies ran while one was open for 14% -> 12% of each run, Pallas kernels for 0% -> 23%
where the time goes in v1:
time: 536 us; the launch traced here: 527 us
  starting transfers between devices  155 us (29%)
  waiting for transfers between devices  153 us (29%)
  Pallas kernels  133 us (25%)
  local copies, waits for them, and re-layouts  37.2 us (7%)
  other arithmetic  28.4 us (5%)
  matrix products  17.6 us (3%)
    pallas_call x24, Pallas kernels, run(): pl.pallas_call(kernel, out_shape=[jax.ShapeDtypeStruct(tuple(s), d) for s...  133 us
    ppermute x59, starting transfers between devices, tp_swap(): return lax.ppermute(x, 'tp', [(i, i ^ m) for i in range(TP)])  74.1 us
    ppermute x18, starting transfers between devices, ctx_from(): return lax.ppermute(x, 'ctx', [((i + m) % C, i) for i in range(C)])  63.6 us
    ppermute x59, waiting for transfers between devices, tp_swap(): return lax.ppermute(x, 'tp', [(i, i ^ m) for i in range(TP)])  62.7 us
    ppermute x9, waiting for transfers between devices, ctx_to(): return lax.ppermute(x, 'ctx', [(i, (i + m) % C) for i in range(C)])  30.6 us
    ppermute x2, waiting for transfers between devices, ctx_down(): return lax.ppermute(x, 'ctx', [(i + k, i) for i in range(C - k)])  30.5 us
    ppermute x18, waiting for transfers between devices, ctx_from(): return lax.ppermute(x, 'ctx', [((i + m) % C, i) for i in range(C)])  26.2 us
    dot_general x8, matrix products, mm(): return lax.dot_general(left, right, dims, preferred_element_type=F32)  15.9 us
  transfers between devices with their start and end apart: 115, of which 34 were waited for; matrix products, arithmetic and copies ran while one was open for 12% of the time, Pallas kernels for 23%

profile of v1, /device:TPU:0, one launch (start us, length us, event | category | flops | bytes accessed | tf_op | source)
XLA Modules:
  0.0 526.6 jit_solution(17491294466275412669)
XLA Ops:
  28.7 9.0 %collective-permute-done.13.refs_2_ = bf16[96,576]{1,0:T(8,128)(2,1)S(1)} collective-permute-done((bf16[96,576]{1,0:T(8,128)(2,1)S(1)}, bf16[96,576]{1,0:T(8,128)(2,1)S(1)}, u32[]{:S(2)}, u32[]{:S(2)}) %collective-permute-start.13) | collective-permute-done | bytes 110624 | tf_op jit(solution)/shard_map/ppermute | solution.py:196
  38.3 6.8 %collective-permute-done.23.refs_2_ = bf16[96,576]{1,0:T(8,128)(2,1)S(1)} collective-permute-done((bf16[96,576]{1,0:T(8,128)(2,1)S(1)}, bf16[96,576]{1,0:T(8,128)(2,1)S(1)}, u32[]{:S(2)}, u32[]{:S(2)}) %collective-permute-start.23) | collective-permute-done | bytes 110624 | tf_op jit(solution)/shard_map/ppermute | solution.py:196
  66.9 7.7 %collective-permute-done.36 = bf16[3,64,768]{2,1,0:T(8,128)(2,1)S(1)} collective-permute-done((bf16[3,64,768]{2,1,0:T(8,128)(2,1)S(1)}, bf16[3,64,768]{2,1,0:T(8,128)(2,1)S(1)}, u32[]{:S(2)}, u32[]{:S(2)}) %collective-permute-start.36) | collective-permute-done | bytes 294944 | tf_op jit(solution)/shard_map/ppermute | solution.py:196
  92.0 12.1 %collective-permute-start.35 = (bf16[3,64,768]{2,1,0:T(8,128)(2,1)S(1)}, bf16[3,64,768]{2,1,0:T(8,128)(2,1)S(1)}, u32[]{:S(2)}, u32[]{:S(2)}) collective-permute-start(bf16[3,64,768]{2,1,0:T(8,128)(2,1)S(1)} %constant_dynamic-slice_fusion.1), channel_id=1, source_target_pairs={{4,0},{8,4},{12,8},{0,12},{5,1},{9,5},{13,9},{1,13},{6,2},{10,6},{... | collective-permute-start | bytes 884744 | tf_op jit(solution)/shard_map/ppermute | solution.py:196
  111.9 10.8 %self_attention.1 = (bf16[3,256,192]{2,1,0:T(8,128)(2,1)}, bf16[3,768,192]{2,1,0:T(8,128)(2,1)}, bf16[3,768,192]{2,1,0:T(8,128)(2,1)}, bf16[3,3,256,768]{3,2,1,0...) custom-call(s32[10]{0:T(128)} %stack.68.sc, ...), custom_call_target="tpu_custom_call" | custom-call | flops 2944401408 | bytes 10346496 | tf_op jit(solution)/shard_map/self_attention/pallas_call | solution.py:54
  135.2 14.5 %collective-permute-start.54 = (bf16[96,1536]{1,0:T(8,128)(2,1)S(1)}, bf16[96,1536]{1,0:T(8,128)(2,1)}, u32[]{:S(2)}, u32[]{:S(2)}) collective-permute-start(bf16[96,1536]{1,0:T(8,128)(2,1)S(1)} %pad_maximum_fusion.5.refs_0_), channel_id=1, source_target_pairs={{4,0},{8,4},{12,8},{0,12},{5,1},{9,5},{13,9},{1,13},{6,2},{10,6},{... | collective-permute-start | bytes 884744 | tf_op jit(solution)/shard_map/ppermute | solution.py:196
  150.5 5.4 %rank_rows.1 = (bf16[768,192]{1,0:T(8,128)(2,1)}, bf16[768,192]{1,0:T(8,128)(2,1)}, bf16[768,192]{1,0:T(8,128)(2,1)}, bf16[768,192]{1,0:T(8,128)(2,1)}, bf16[768...) custom-call(s32[10]{0:T(128)} %stack.68.sc, ...), custom_call_target="tpu_custom_call" | custom-call | bytes 7077888 | tf_op jit(solution)/shard_map/rank_rows/pallas_call | solution.py:54
  172.4 13.1 %collective-permute-start.56 = (bf16[96,1536]{1,0:T(8,128)(2,1)S(1)}, bf16[96,1536]{1,0:T(8,128)(2,1)S(1)}, u32[]{:S(2)}, u32[]{:S(2)}) collective-permute-start(bf16[96,1536]{1,0:T(8,128)(2,1)S(1)} %pad_maximum_fusion.5.refs_0_), channel_id=1, source_target_pairs={{12,0},{0,4},{4,8},{8,12},{13,1},{1,5},{5,9},{9,13},{14,2},{2,6},{... | collective-permute-start | bytes 884744 | tf_op jit(solution)/shard_map/ppermute | solution.py:196
  188.2 7.1 %cross_keys.1 = (bf16[3,1024,192]{2,1,0:T(8,128)(2,1)}, bf16[3,1024,192]{2,1,0:T(8,128)(2,1)}) custom-call(s32[10]{0:T(128)} %stack.68.sc, bf16[3,256,768]{2,1,0:T(8,128)(2,1)} %refs_0_.5, bf16[3,3,64,768]{3,2,1,0:T(8,128)(2,1)} %copy-done.17, bf16[3,3,64,768]{3,2,1,0:T(8,128)(2,1)} %collective-permute-done.38.refs_2_, ...), custom_call_target="tpu_custom_call" | custom-call | flops 1811939328 | bytes 7667712 | tf_op jit(solution)/shard_map/cross_keys/pallas_call | solution.py:54
  196.0 8.6 %cross_attention.1 = (bf16[3,256,192]{2,1,0:T(8,128)(2,1)}, bf16[3,3,256,1024]{3,2,1,0:T(8,128)(2,1)}, bf16[3,64,192]{2,1,0:T(8,128)(2,1)}, bf16[3,64,192]{2,1,0...) custom-call(s32[10]{0:T(128)} %stack.68.sc, bf16[3,64,192]{2,1,0:T(8,128)(2,1)} %bitcast.162, ...), custom_call_target="tpu_custom_call" | custom-call | flops 1811939328 | bytes 7977984 | tf_op jit(solution)/shard_map/cross_attention/pallas_call | solution.py:54
  226.9 6.8 %collective-permute-done.52.refs_2_ = bf16[3,64,768]{2,1,0:T(8,128)(2,1)S(1)} collective-permute-done((bf16[3,64,768]{2,1,0:T(8,128)(2,1)}, bf16[3,64,768]{2,1,0:T(8,128)(2,1)S(1)}, u32[]{:S(2)}, u32[]{:S(2)}) %collective-permute-start.52) | collective-permute-done | bytes 294944 | tf_op jit(solution)/shard_map/ppermute | solution.py:190
  234.6 9.2 %feed_forward.1 = (bf16[3,256,768]{2,1,0:T(8,128)(2,1)}, bf16[3,256,512]{2,1,0:T(8,128)(2,1)}, bf16[3,256,1024]{2,1,0:T(8,128)(2,1)}, f32[3,64,768]{2,1,0:T(8,12...) custom-call(s32[10]{0:T(128)} %stack.68.sc, ...), custom_call_target="tpu_custom_call" | custom-call | flops 3623878656 | bytes 12386304 | tf_op jit(solution)/shard_map/feed_forward/pallas_call | solution.py:54
  266.7 6.1 %collective-permute-done.68 = bf16[3,64,768]{2,1,0:T(8,128)(2,1)S(1)} collective-permute-done((bf16[3,64,768]{2,1,0:T(8,128)(2,1)}, bf16[3,64,768]{2,1,0:T(8,128)(2,1)S(1)}, u32[]{:S(2)}, u32[]{:S(2)}) %collective-permute-start.68) | collective-permute-done | bytes 294944 | tf_op jit(solution)/shard_map/ppermute | solution.py:190
  286.9 11.8 %cross_backward.1 = (bf16[3,64,192]{2,1,0:T(8,128)(2,1)}, bf16[3,64,192]{2,1,0:T(8,128)(2,1)}, bf16[3,64,192]{2,1,0:T(8,128)(2,1)}, bf16[3,64,192]{2,1,0:T(8,128...) custom-call(s32[10]{0:T(128)} %stack.68.sc, ...), custom_call_target="tpu_custom_call" | custom-call | flops 3623878656 | bytes 10911744 | tf_op jit(solution)/shard_map/cross_backward/pallas_call | solution.py:54
  306.7 5.3 grad_one.1
  325.9 11.3 %self_backward.1 = (bf16[3,256,192]{2,1,0:T(8,128)(2,1)}, f32[3,256,384]{2,1,0:T(8,128)}, bf16[3,256,384]{2,1,0:T(8,128)(2,1)}, bf16[3,256,384]{2,1,0:T(8,128)(2,1)}, f32[3,1024]{1,0:T(4,128)}) custom-call(s32[10]{0:T(128)} %stack.68.sc, bf16[3,64,192]{2,1,0:T(8,128)(2,1)} %bitcast.164, bf16[3,64,192]{2,1,0:T(8,128)(2,1)} %bitcast.166, ...), custom_call_target="tpu_custom_call" | custom-call | flops 2717908992 | bytes 8564736 | tf_op jit(solution)/shard_map/self_backward/pallas_call | solution.py:54
  348.4 5.5 %encoder_back.1 = (bf16[3,256,384]{2,1,0:T(8,128)(2,1)}, f32[3,64,768]{2,1,0:T(8,128)}, bf16[3,64,768]{2,1,0:T(8,128)(2,1)}, bf16[3,64,768]{2,1,0:T(8,128)(2,1)}, bf16[3,64,768]{2,1,0:T(8,128)(2,1)}) custom-call(s32[10]{0:T(128)} %stack.68.sc, f32[3,256,384]{2,1,0:T(8,128)} %get-tuple-element.190.refs_0_, ...), custom_call_target="tpu_custom_call" | custom-call | flops 452984832 | bytes 5603328 | tf_op jit(solution)/shard_map/encoder_back/pallas_call | solution.py:54
  373.0 25.8 %collective-permute-done.80.refs_3_ = bf16[3,256,384]{2,1,0:T(8,128)(2,1)} collective-permute-done((bf16[3,256,384]{2,1,0:T(8,128)(2,1)S(1)}, bf16[3,256,384]{2,1,0:T(8,128)(2,1)}, u32[]{:S(2)}, u32[]{:S(2)}) %collective-permute-start.80) | collective-permute-done | bytes 589856 | tf_op jit(solution)/shard_map/ppermute | solution.py:205
  398.8 5.6 %self_projections_back.1 = (bf16[3,256,384]{2,1,0:T(8,128)(2,1)}, f32[3,64,768]{2,1,0:T(8,128)}, bf16[3,64,768]{2,1,0:T(8,128)(2,1)}, bf16[3,64,768]{2,1,0:T(8,128)(2,1)}, bf16[3,64,768]{2,1,0:T(8,128)(2,1)}) custom-call(s32[10]{0:T(128)} %stack.68.sc, bf16[3,256,192]{2,1,0:T(8,128)(2,1)} %get-tuple-element.180.refs_0_, ...), custom_call_target="tpu_custom_call" | custom-call | flops 679477248 | bytes 5603328 | tf_op jit(solution)/shard_map/self_projections_back/pallas_call | solution.py:54
  417.7 6.9 %collective-permute-start.92 = (bf16[3,64,768]{2,1,0:T(8,128)(2,1)}, bf16[3,64,768]{2,1,0:T(8,128)(2,1)}, u32[]{:S(2)}, u32[]{:S(2)}) collective-permute-start(bf16[3,64,768]{2,1,0:T(8,128)(2,1)} %get-tuple-element.197), channel_id=1, source_target_pairs={{0,3},{1,2},{2,1},{3,0},{4,7},{5,6},{6,5},{7,4},{8,11},{9,10},{10,... | collective-permute-start | bytes 884744 | tf_op jit(solution)/shard_map/ppermute | solution.py:190
  454.1 7.3 %collective-permute-done.105 = bf16[384,576]{0,1:T(8,128)(2,1)S(1)} collective-permute-done((bf16[384,576]{0,1:T(8,128)(2,1)S(1)}, bf16[384,576]{0,1:T(8,128)(2,1)S(1)}, u32[]{:S(2)}, u32[]{:S(2)}) %collective-permute-start.105) | collective-permute-done | bytes 442400 | tf_op jit(solution)/shard_map/ppermute | solution.py:190
  464.7 14.7 %collective-permute-done.113 = bf16[96,1536]{1,0:T(8,128)(2,1)} collective-permute-done((bf16[96,1536]{1,0:T(8,128)(2,1)}, bf16[96,1536]{1,0:T(8,128)(2,1)}, u32[]{:S(2)}, u32[]{:S(2)}) %collective-permute-start.113) | collective-permute-done | bytes 294944 | tf_op jit(solution)/shard_map/ppermute | solution.py:199
  490.2 5.3 %collective-permute-done.84.refs_1_ = bf16[3,64,768]{2,1,0:T(8,128)(2,1)S(1)} collective-permute-done((bf16[3,64,768]{2,1,0:T(8,128)(2,1)}, bf16[3,64,768]{2,1,0:T(8,128)(2,1)S(1)}, u32[]{:S(2)}, u32[]{:S(2)}) %collective-permute-start.84) | collective-permute-done | bytes 294944 | tf_op jit(solution)/shard_map/ppermute | solution.py:190
  506.2 13.4 %collective-permute-done.109 = bf16[96,1536]{0,1:T(8,128)(2,1)S(1)} collective-permute-done((bf16[96,1536]{0,1:T(8,128)(2,1)}, bf16[96,1536]{0,1:T(8,128)(2,1)S(1)}, u32[]{:S(2)}, u32[]{:S(2)}) %collective-permute-start.109) | collective-permute-done | bytes 294944 | tf_op jit(solution)/shard_map/ppermute | solution.py:199
  (564 shorter events, 293.9 us)
Async XLA Ops:
  79.5 28.2 %collective-permute-start.10 = (bf16[3,64,768]{2,1,0:T(8,128)(2,1)}, bf16[3,64,768]{2,1,0:T(8,128)(2,1)}, u32[]{:S(2)}, u32[]{:S(2)}) collective-permute-start(bf16[3,64,768]{2,1,0:T(8,128)(2,1)} %collective-permute-done.8.refs_5_), channel_id=1, source_target_pairs={{0,2},{1,3},{2,0},{3,1},{4,6},{5,7},{6,4},{7,5},{8,10},{9,11},{10,... | collective-permute-start | bytes 884744 | tf_op jit(solution)/shard_map/ppermute | solution.py:190
  81.1 30.3 %collective-permute-start.11 = (bf16[3,64,768]{2,1,0:T(8,128)(2,1)}, bf16[3,64,768]{2,1,0:T(8,128)(2,1)}, u32[]{:S(2)}, u32[]{:S(2)}) collective-permute-start(bf16[3,64,768]{2,1,0:T(8,128)(2,1)} %collective-permute-done.8.refs_5_), channel_id=1, source_target_pairs={{0,3},{1,2},{2,1},{3,0},{4,7},{5,6},{6,5},{7,4},{8,11},{9,10},{10,... | collective-permute-start | bytes 884744 | tf_op jit(solution)/shard_map/ppermute | solution.py:190
  82.5 40.4 %collective-permute-start.26 = (bf16[384,576]{1,0:T(8,128)(2,1)}, bf16[384,576]{1,0:T(8,128)(2,1)S(1)}, u32[]{:S(2)}, u32[]{:S(2)}) collective-permute-start(bf16[384,576]{1,0:T(8,128)(2,1)} %half_rows.1.refs_0_), channel_id=1, source_target_pairs={{0,2},{1,3},{2,0},{3,1},{4,6},{5,7},{6,4},{7,5},{8,10},{9,11},{10,... | collective-permute-start | bytes 1327112 | tf_op jit(solution)/shard_map/ppermute | solution.py:190
  85.6 39.8 %collective-permute-start.27 = (bf16[384,576]{1,0:T(8,128)(2,1)}, bf16[384,576]{1,0:T(8,128)(2,1)S(1)}, u32[]{:S(2)}, u32[]{:S(2)}) collective-permute-start(bf16[384,576]{1,0:T(8,128)(2,1)} %half_rows.1.refs_0_), channel_id=1, source_target_pairs={{0,3},{1,2},{2,1},{3,0},{4,7},{5,6},{6,5},{7,4},{8,11},{9,10},{10,... | collective-permute-start | bytes 1327112 | tf_op jit(solution)/shard_map/ppermute | solution.py:190
  92.0 30.8 %collective-permute-start.35 = (bf16[3,64,768]{2,1,0:T(8,128)(2,1)S(1)}, bf16[3,64,768]{2,1,0:T(8,128)(2,1)S(1)}, u32[]{:S(2)}, u32[]{:S(2)}) collective-permute-start(bf16[3,64,768]{2,1,0:T(8,128)(2,1)S(1)} %constant_dynamic-slice_fusion.1), channel_id=1, source_target_pairs={{4,0},{8,4},{12,8},{0,12},{5,1},{9,5},{13,9},{1,13},{6,2},{10,6},{... | collective-permute-start | bytes 884744 | tf_op jit(solution)/shard_map/ppermute | solution.py:196
  127.7 57.9 %collective-permute-start.38 = (bf16[3,3,64,768]{3,2,1,0:T(8,128)(2,1)S(1)}, bf16[3,3,64,768]{3,2,1,0:T(8,128)(2,1)}, u32[]{:S(2)}, u32[]{:S(2)}) collective-permute-start(bf16[3,3,64,768]{3,2,1,0:T(8,128)(2,1)S(1)} %pad_maximum_fusion.1.refs_1_), channel_id=1, source_target_pairs={{0,1},{1,0},{2,3},{3,2},{4,5},{5,4},{6,7},{7,6},{8,9},{9,8},{10,11... | collective-permute-start | bytes 2654216 | tf_op jit(solution)/shard_map/ppermute | solution.py:190
  128.3 57.2 %collective-permute-start.39 = (bf16[3,3,64,768]{3,2,1,0:T(8,128)(2,1)S(1)}, bf16[3,3,64,768]{3,2,1,0:T(8,128)(2,1)}, u32[]{:S(2)}, u32[]{:S(2)}) collective-permute-start(bf16[3,3,64,768]{3,2,1,0:T(8,128)(2,1)S(1)} %pad_maximum_fusion.1.refs_1_), channel_id=1, source_target_pairs={{0,2},{1,3},{2,0},{3,1},{4,6},{5,7},{6,4},{7,5},{8,10},{9,11},{10,... | collective-permute-start | bytes 2654216 | tf_op jit(solution)/shard_map/ppermute | solution.py:190
  130.3 55.8 %collective-permute-start.40 = (bf16[3,3,64,768]{3,2,1,0:T(8,128)(2,1)S(1)}, bf16[3,3,64,768]{3,2,1,0:T(8,128)(2,1)}, u32[]{:S(2)}, u32[]{:S(2)}) collective-permute-start(bf16[3,3,64,768]{3,2,1,0:T(8,128)(2,1)S(1)} %pad_maximum_fusion.1.refs_1_), channel_id=1, source_target_pairs={{0,3},{1,2},{2,1},{3,0},{4,7},{5,6},{6,5},{7,4},{8,11},{9,10},{10,... | collective-permute-start | bytes 2654216 | tf_op jit(solution)/shard_map/ppermute | solution.py:190
  135.2 26.8 %collective-permute-start.54 = (bf16[96,1536]{1,0:T(8,128)(2,1)S(1)}, bf16[96,1536]{1,0:T(8,128)(2,1)}, u32[]{:S(2)}, u32[]{:S(2)}) collective-permute-start(bf16[96,1536]{1,0:T(8,128)(2,1)S(1)} %pad_maximum_fusion.5.refs_0_), channel_id=1, source_target_pairs={{4,0},{8,4},{12,8},{0,12},{5,1},{9,5},{13,9},{1,13},{6,2},{10,6},{... | collective-permute-start | bytes 884744 | tf_op jit(solution)/shard_map/ppermute | solution.py:196
  170.0 35.5 %collective-permute-start.55 = (bf16[96,1536]{1,0:T(8,128)(2,1)S(1)}, bf16[96,1536]{1,0:T(8,128)(2,1)S(1)}, u32[]{:S(2)}, u32[]{:S(2)}) collective-permute-start(bf16[96,1536]{1,0:T(8,128)(2,1)S(1)} %pad_maximum_fusion.5.refs_0_), channel_id=1, source_target_pairs={{8,0},{12,4},{0,8},{4,12},{9,1},{13,5},{1,9},{5,13},{10,2},{14,6},... | collective-permute-start | bytes 884744 | tf_op jit(solution)/shard_map/ppermute | solution.py:196
  172.4 33.7 %collective-permute-start.56 = (bf16[96,1536]{1,0:T(8,128)(2,1)S(1)}, bf16[96,1536]{1,0:T(8,128)(2,1)S(1)}, u32[]{:S(2)}, u32[]{:S(2)}) collective-permute-start(bf16[96,1536]{1,0:T(8,128)(2,1)S(1)} %pad_maximum_fusion.5.refs_0_), channel_id=1, source_target_pairs={{12,0},{0,4},{4,8},{8,12},{13,1},{1,5},{5,9},{9,13},{14,2},{2,6},{... | collective-permute-start | bytes 884744 | tf_op jit(solution)/shard_map/ppermute | solution.py:196
  185.5 32.5 %collective-permute-start.57 = (bf16[96,1536]{1,0:T(8,128)(2,1)S(1)}, bf16[96,1536]{1,0:T(8,128)(2,1)S(1)}, u32[]{:S(2)}, u32[]{:S(2)}) collective-permute-start(bf16[96,1536]{1,0:T(8,128)(2,1)S(1)} %pad_maximum_fusion.5.refs_0_), channel_id=1, source_target_pairs={{0,16},{16,0},{1,17},{17,1},{2,18},{18,2},{3,19},{19,3},{4,20},{20... | collective-permute-start | bytes 884744 | tf_op jit(solution)/shard_map/ppermute | solution.py:193
  185.6 33.5 %collective-permute-start.58 = (bf16[96,1536]{1,0:T(8,128)(2,1)}, bf16[96,1536]{1,0:T(8,128)(2,1)S(1)}, u32[]{:S(2)}, u32[]{:S(2)}) collective-permute-start(bf16[96,1536]{1,0:T(8,128)(2,1)} %collective-permute-done.54.refs_1_), channel_id=1, source_target_pairs={{0,16},{16,0},{1,17},{17,1},{2,18},{18,2},{3,19},{19,3},{4,20},{20... | collective-permute-start | bytes 884744 | tf_op jit(solution)/shard_map/ppermute | solution.py:193
  265.0 59.9 %collective-permute-start.64 = (bf16[3,64,768]{2,1,0:T(8,128)(2,1)}, bf16[3,64,768]{2,1,0:T(8,128)(2,1)S(1)}, u32[]{:S(2)}, u32[]{:S(2)}) collective-permute-start(bf16[3,64,768]{2,1,0:T(8,128)(2,1)} %bitcast.107), channel_id=1, source_target_pairs={{0,1},{1,0},{2,3},{3,2},{4,5},{5,4},{6,7},{7,6},{8,9},{9,8},{10,11... | collective-permute-start | bytes 884744 | tf_op jit(solution)/shard_map/ppermute | solution.py:190
  266.2 71.1 %collective-permute-start.65 = (bf16[3,64,768]{2,1,0:T(8,128)(2,1)}, bf16[3,64,768]{2,1,0:T(8,128)(2,1)}, u32[]{:S(2)}, u32[]{:S(2)}) collective-permute-start(bf16[3,64,768]{2,1,0:T(8,128)(2,1)} %bitcast.108), channel_id=1, source_target_pairs={{0,2},{1,3},{2,0},{3,1},{4,6},{5,7},{6,4},{7,5},{8,10},{9,11},{10,... | collective-permute-start | bytes 884744 | tf_op jit(solution)/shard_map/ppermute | solution.py:190
  304.4 34.4 %collective-permute-start.87 = (bf16[3,256,384]{2,1,0:T(8,128)(2,1)}, bf16[3,256,384]{2,1,0:T(8,128)(2,1)}, u32[]{:S(2)}, u32[]{:S(2)}) collective-permute-start(bf16[3,256,384]{2,1,0:T(8,128)(2,1)} %get-tuple-element.191), channel_id=1, source_target_pairs={{0,4},{4,8},{8,12},{12,0},{1,5},{5,9},{9,13},{13,1},{2,6},{6,10},{... | collective-permute-start | bytes 1769480 | tf_op jit(solution)/shard_map/ppermute | solution.py:199
  347.1 91.2 %collective-permute-start.111 = (bf16[384,1536]{1,0:T(8,128)(2,1)}, bf16[384,1536]{1,0:T(8,128)(2,1)}, u32[]{:S(2)}, u32[]{:S(2)}) collective-permute-start(bf16[384,1536]{1,0:T(8,128)(2,1)} %fusion.1), channel_id=1, source_target_pairs={{0,16},{16,0},{1,17},{17,1},{2,18},{18,2},{3,19},{19,3},{4,20},{20... | collective-permute-start | bytes 3538952 | tf_op jit(solution)/shard_map/ppermute | solution.py:193
  357.2 41.6 %collective-permute-start.80 = (bf16[3,256,384]{2,1,0:T(8,128)(2,1)S(1)}, bf16[3,256,384]{2,1,0:T(8,128)(2,1)}, u32[]{:S(2)}, u32[]{:S(2)}) collective-permute-start(bf16[3,256,384]{2,1,0:T(8,128)(2,1)S(1)} %copy-done.98), channel_id=1, source_target_pairs={{8,0},{12,4},{9,1},{13,5},{10,2},{14,6},{11,3},{15,7},{24,16},{28,... | collective-permute-start | bytes 1769480 | tf_op jit(solution)/shard_map/ppermute | solution.py:205
  361.6 81.6 %collective-permute-start.90 = (bf16[3,64,768]{2,1,0:T(8,128)(2,1)}, bf16[3,64,768]{2,1,0:T(8,128)(2,1)}, u32[]{:S(2)}, u32[]{:S(2)}) collective-permute-start(bf16[3,64,768]{2,1,0:T(8,128)(2,1)} %get-tuple-element.195), channel_id=1, source_target_pairs={{0,1},{1,0},{2,3},{3,2},{4,5},{5,4},{6,7},{7,6},{8,9},{9,8},{10,11... | collective-permute-start | bytes 884744 | tf_op jit(solution)/shard_map/ppermute | solution.py:190
  416.7 28.1 %collective-permute-start.91 = (bf16[3,64,768]{2,1,0:T(8,128)(2,1)}, bf16[3,64,768]{2,1,0:T(8,128)(2,1)}, u32[]{:S(2)}, u32[]{:S(2)}) collective-permute-start(bf16[3,64,768]{2,1,0:T(8,128)(2,1)} %get-tuple-element.196), channel_id=1, source_target_pairs={{0,2},{1,3},{2,0},{3,1},{4,6},{5,7},{6,4},{7,5},{8,10},{9,11},{10,... | collective-permute-start | bytes 884744 | tf_op jit(solution)/shard_map/ppermute | solution.py:190
  417.7 28.9 %collective-permute-start.92 = (bf16[3,64,768]{2,1,0:T(8,128)(2,1)}, bf16[3,64,768]{2,1,0:T(8,128)(2,1)}, u32[]{:S(2)}, u32[]{:S(2)}) collective-permute-start(bf16[3,64,768]{2,1,0:T(8,128)(2,1)} %get-tuple-element.197), channel_id=1, source_target_pairs={{0,3},{1,2},{2,1},{3,0},{4,7},{5,6},{6,5},{7,4},{8,11},{9,10},{10,... | collective-permute-start | bytes 884744 | tf_op jit(solution)/shard_map/ppermute | solution.py:190
  446.7 32.7 %collective-permute-start.107 = (bf16[384,960]{0,1:T(8,128)(2,1)S(1)}, bf16[384,960]{0,1:T(8,128)(2,1)}, u32[]{:S(2)}, u32[]{:S(2)}) collective-permute-start(bf16[384,960]{0,1:T(8,128)(2,1)S(1)} %dynamic-slice_convert_fusion), channel_id=1, source_target_pairs={{0,16},{16,0},{1,17},{17,1},{2,18},{18,2},{3,19},{19,3},{4,20},{20... | collective-permute-start | bytes 2211848 | tf_op jit(solution)/shard_map/ppermute | solution.py:193
  453.0 26.3 %collective-permute-start.113 = (bf16[96,1536]{1,0:T(8,128)(2,1)}, bf16[96,1536]{1,0:T(8,128)(2,1)}, u32[]{:S(2)}, u32[]{:S(2)}) collective-permute-start(bf16[96,1536]{1,0:T(8,128)(2,1)} %get-tuple-element.260), channel_id=1, source_target_pairs={{0,8},{4,12},{8,0},{12,4},{1,9},{5,13},{9,1},{13,5},{2,10},{6,14},... | collective-permute-start | bytes 884744 | tf_op jit(solution)/shard_map/ppermute | solution.py:199
  490.2 29.5 %collective-permute-start.109 = (bf16[96,1536]{0,1:T(8,128)(2,1)}, bf16[96,1536]{0,1:T(8,128)(2,1)S(1)}, u32[]{:S(2)}, u32[]{:S(2)}) collective-permute-start(bf16[96,1536]{0,1:T(8,128)(2,1)} %get-tuple-element.262), channel_id=1, source_target_pairs={{0,8},{4,12},{8,0},{12,4},{1,9},{5,13},{9,1},{13,5},{2,10},{6,14},... | collective-permute-start | bytes 884744 | tf_op jit(solution)/shard_map/ppermute | solution.py:199
  (205 other events, 2559.6 us)
